TPU v7x, 256 devices: a whole 4x4x8 slice. The times are simulated.
256 devices in a mesh: tm: 8 (over z), lat: 32 (over y, x, core).
Axes of the slice: x: 4, y: 4, z: 8, core: 2. Of those that a mesh axis runs over, the one named last changes fastest.
Arguments:
- wind_east: bfloat16 [960, 256, 1440], P('tm', 'lat'), may hold values from -40 to 40
- wind_north: bfloat16 [960, 256, 1440], P('tm', 'lat'), may hold values from -40 to 40
- snap_counts: int32 [8], P('tm'), may hold values from 1 to 120, 320 in all
- snap_ids: int32 [960], P('tm'), may hold values from 0 to 8759
Outputs:
- basis: bfloat16 [32, 256, 1440], P(None, 'lat')
- coeffs: float32 [32, 960], P(None, 'tm')
Inputs may be any that keep to these rules, and one draw needn't show every extreme that they name: `snap_counts`: entry b counts the used slots of the b-th block of 120 slots, which are that block's first ones; the entries sum to 320 and one of them equals 120.
All inputs are finite; a program needn't handle non-finite values.
Results may differ from a plain program's by a relative error of at most 0.0072.
Values may be sent and summed in bfloat16 or wider, within the bound.
A program may use at most 64 MiB of HBM per device.

v0:
```python
import jax
import jax.numpy as jnp
from jax import lax
from jax.sharding import PartitionSpec as P

RANK = 32


def with_halo(cells, sides, width):
    for axis, dim in sides:
        count = lax.axis_size(axis)
        ends = count - 1
        head = lax.slice_in_dim(cells, 0, width, axis=dim)
        tail = lax.slice_in_dim(cells, cells.shape[dim] - width, cells.shape[dim], axis=dim)
        cells = jnp.concatenate(
            [
                lax.ppermute(tail, axis, [(i, (i + 1) % count) for i in range(ends)]),
                cells,
                lax.ppermute(head, axis, [((i + 1) % count, i) for i in range(ends)]),
            ],
            axis=dim,
        )
    return cells


def latitude_cosine(first_row, row_count, total_rows):
    row_index = first_row + jnp.arange(row_count, dtype=jnp.int32)
    return jnp.cos((total_rows // 2 - row_index).astype(jnp.float32) * (jnp.pi / 720.0))


def sign_table(snap_ids, rank_count):
    column = jnp.arange(rank_count, dtype=jnp.int32)
    mixed = snap_ids[:, None] * 1103515245 + column[None, :] * 40503 + 12345
    mixed = jnp.bitwise_xor(mixed, jnp.right_shift(mixed, 13))
    mixed = mixed * 1664525 + 1013904223
    mixed = jnp.bitwise_xor(mixed, jnp.right_shift(mixed, 16))
    flipped = jnp.bitwise_and(jnp.right_shift(mixed, 7), 1)
    return (1 - 2 * flipped).astype(jnp.bfloat16)


def metric_vorticity(padded_east, wind_north, padded_cosine, valid):
    scaled = padded_east.astype(jnp.float32) * padded_cosine[None, :, None]
    north_side = scaled[:, :-2]
    south_side = scaled[:, 2:]
    meridional = wind_north.astype(jnp.float32)
    zonal_diff = jnp.roll(meridional, -1, axis=2) - jnp.roll(meridional, 1, axis=2)
    weight = 0.5 / jnp.sqrt(padded_cosine[1:-1])
    field = (zonal_diff - north_side + south_side) * weight[None, :, None] * valid[:, None, None]
    return field.astype(jnp.bfloat16)


def local_gram(sketch, cell_total):
    return (
        lax.dot_general(
            sketch,
            sketch,
            (((1,), (1,)), ((), ())),
            precision=lax.Precision.HIGHEST,
            preferred_element_type=jnp.float32,
        )
        / cell_total
    )


def orthonormal(gram_sum, sketch):
    factor = jnp.linalg.cholesky(gram_sum)
    inverse = lax.linalg.triangular_solve(
        factor, jnp.eye(gram_sum.shape[0], dtype=jnp.float32), left_side=True, lower=True
    )
    return jnp.dot(
        inverse, sketch, precision=lax.Precision.HIGHEST, preferred_element_type=jnp.float32
    ).astype(jnp.bfloat16)


def local(wind_east, wind_north, snap_counts, snap_ids):
    snap_slots, band_rows, lon_count = wind_east.shape
    band_count = lax.axis_size("lat")
    first_row = lax.axis_index("lat") * band_rows - 1
    padded_cosine = latitude_cosine(first_row, band_rows + 2, band_rows * band_count)
    valid = (jnp.arange(snap_slots, dtype=jnp.int32) < snap_counts[0]).astype(jnp.float32)
    padded_east = with_halo(wind_east, (("lat", 1),), 1)
    field = metric_vorticity(padded_east, wind_north, padded_cosine, valid).reshape(
        snap_slots, band_rows * lon_count
    )
    signs_matrix = sign_table(snap_ids, RANK)
    sketch = jnp.dot(signs_matrix.T, field, preferred_element_type=jnp.float32)
    cell_total = band_rows * band_count * lon_count
    sketch = lax.psum(sketch, "tm")
    gram_sum = lax.psum(local_gram(sketch, cell_total), "lat")
    basis_flat = orthonormal(gram_sum, sketch)
    projected = (
        lax.dot_general(
            basis_flat, field, (((1,), (1,)), ((), ())), preferred_element_type=jnp.float32
        )
        / cell_total
    )
    coeffs = lax.psum(projected, "lat")
    return (basis_flat.reshape(basis_flat.shape[0], band_rows, lon_count), coeffs)


def solution(mesh):
    in_specs = (P("tm", "lat", None), P("tm", "lat", None), P("tm"), P("tm"))
    out_specs = (P(None, "lat", None), P(None, "tm"))
    return jax.shard_map(local, mesh=mesh, in_specs=in_specs, out_specs=out_specs, check_vma=False)
```

profile of v0, /device:TPU:1, one launch (start us, length us, event | category | flops | bytes accessed | tf_op | source)
XLA Modules:
  0.0 395.5 jit_solution(5653867448975015679)
XLA Ops:
  7.2 0.0 copy-start
  7.2 0.0 all-reduce.2.cloned.1.call-start
  7.2 4.0 %fusion.36 = (bf16[120,1,1440]{2,1,0:T(2,128)(2,1)S(1)}, bf16[120,1,1440]{2,1,0:T(2,128)(2,1)S(1)}) fusion(bf16[120,8,1440]{2,1,0:T(8,128)(2,1)} %param.4), kind=kLoop, calls=%fused_computation.55 | loop fusion | bytes 1382400 | tf_op jit(solution)/shard_map/slice | solution.py:14
  11.2 0.8 copy.21
  12.0 4.5 %collective-permute-start = (bf16[120,1,1440]{2,0,1:T(8,128)(2,1)}, bf16[120,1,1440]{2,0,1:T(8,128)(2,1)}, u32[]{:S(2)}, u32[]{:S(2)}) collective-permute-start(bf16[120,1,1440]{2,0,1:T(8,128)(2,1)} %copy.21), channel_id=1, source_target_pairs={{0,1},{1,2},{2,3},{3,4},{4,5},{5,6},{6,7},{7,8},{8,9},{9,10},{10,1... | collective-permute-start | bytes 1036808 | tf_op jit(solution)/shard_map/ppermute | solution.py:17
  16.5 0.8 copy.22
  17.3 2.7 collective-permute-start.1
  20.1 0.0 copy-done
  20.1 0.0 copy-start.3
  20.1 6.0 %fusion.35 = (f32[120,8,1439]{2,1,0:T(8,128)}, f32[120,8,1439]{2,1,0:T(8,128)}) fusion(bf16[120,8,1440]{2,1,0:T(8,128)(2,1)S(1)} %copy-done), kind=kLoop, calls=%fused_computation.54 | loop fusion | bytes 22103040 | tf_op jit(solution)/shard_map/jit(_roll_static)/slice | solution.py:46
  26.1 0.0 copy-start.1
  26.1 0.1 rsqrt_multiply_fusion
  26.9 0.0 copy-done.3
  27.0 0.9 fusion.34
  27.8 0.0 collective-permute-done
  27.9 1.6 copy.16
  29.4 0.0 collective-permute-done.1
  29.4 0.0 slice-start
  29.4 1.7 copy.17
  31.1 0.0 copy-done.1
  31.2 0.0 slice-start.1
  31.2 0.0 copy-start.2
  31.2 3.5 convert_multiply_fusion
  34.7 0.0 slice-done
  34.7 0.0 slice-done.1
  34.7 0.0 copy-done.2
  34.7 6.7 %fusion.2 = bf16[120,8,1440]{2,1,0:T(8,128)(2,1)} fusion(f32[120,10,1440]{2,1,0:T(8,128)S(1)} %convert_multiply_fusion, f32[120,8,1]{2,1,0:T(8,128)S(1)} %copy-done.2, f32[120,8,1439]{2,1,0:T(8,128)} %get-tuple-element.5, f32[120,8,1439]{2,1,0:T(8,128)S(1)} %bitcast.19, f32[120,8,1]{2,1,0:T(8,128)S(1)} %get-tuple-element.2, f32[120]{0:T(128)S(1)} %compare_convert_fusion, ...), kind=kLoop, calls=%fused_computation.5 | loop fusion | flops 11059200 | bytes 24883712 | tf_op jit(solution)/shard_map/convert_element_type | solution.py:49
  41.4 5.6 %reshape.40 = bf16[120,11520]{1,0:T(8,128)(2,1)S(1)} reshape(bf16[120,8,1440]{2,1,0:T(8,128)(2,1)} %fusion.2) | data formatting | bytes 5529600 | tf_op jit(solution)/shard_map/reshape | solution.py:82
  47.0 1.7 fusion.14
  48.7 0.0 all-reduce.2.cloned.1.call-update
  48.7 76.9 %all-reduce.2.cloned.1.call-done = f32[32,11520]{1,0:T(8,128)} async-done(((f32[32,11520]{1,0:T(8,128)}), f32[32,11520]{1,0:T(8,128)}) %all-reduce.2.cloned.1.call-update) | async-done | bytes 1474576 | tf_op jit(solution)/shard_map/psum | solution.py:88
  125.6 3.2 convolution_multiply_fusion.1
  128.8 123.2 %psum.22 = f32[32,32]{0,1:T(8,128)S(1)} all-reduce(f32[32,32]{0,1:T(8,128)S(1)} %convolution_multiply_fusion.1), channel_id=1, replica_groups=mesh['tm'=8,'lat'=32] {'lat'}, use_global_device_ids=true, to_apply=%region_1.2 | all-reduce | flops 1024 | bytes 8192 | tf_op jit(solution)/shard_map/psum | solution.py:89
  252.1 0.1 copy.19
  252.1 2.9 cholesky.17
  255.1 0.6 compare_reduce_fusion
  255.7 0.7 fusion.3
  256.4 2.4 custom-call.6
  258.8 0.2 fusion.11
  259.0 2.7 convolution_convert_fusion
  261.8 0.9 convolution_multiply_fusion
  262.7 2.1 reshape.41
  264.8 123.8 %psum.23 = f32[32,120]{1,0:T(8,128)} all-reduce(f32[32,120]{1,0:T(8,128)S(1)} %convolution_multiply_fusion), channel_id=1, replica_groups=mesh['tm'=8,'lat'=32] {'lat'}, use_global_device_ids=true, to_apply=%region_4.5 | all-reduce | flops 3840 | bytes 30720 | tf_op jit(solution)/shard_map/psum | solution.py:97
  (7 shorter events, 0.1 us)
Async XLA Ops:
  7.2 12.9 %copy-start = (bf16[120,8,1440]{2,1,0:T(8,128)(2,1)S(1)}, bf16[120,8,1440]{2,1,0:T(8,128)(2,1)}, u32[]{:S(2)}) copy-start(bf16[120,8,1440]{2,1,0:T(8,128)(2,1)} %param.5) | copy-start | bytes 8294404
  7.2 118.5 %all-reduce.2.cloned.1.call-start = ((), (), s32[]{:S(2)}) async-start(), calls=%async_computation | async-start | bytes 2949120 | tf_op jit(solution)/shard_map/psum | solution.py:88
  12.0 15.8 %collective-permute-start = (bf16[120,1,1440]{2,0,1:T(8,128)(2,1)}, bf16[120,1,1440]{2,0,1:T(8,128)(2,1)}, u32[]{:S(2)}, u32[]{:S(2)}) collective-permute-start(bf16[120,1,1440]{2,0,1:T(8,128)(2,1)} %copy.21), channel_id=1, source_target_pairs={{0,1},{1,2},{2,3},{3,4},{4,5},{5,6},{6,7},{7,8},{8,9},{9,10},{10,1... | collective-permute-start | bytes 1036808 | tf_op jit(solution)/shard_map/ppermute | solution.py:17
  17.3 12.1 %collective-permute-start.1 = (bf16[120,1,1440]{2,0,1:T(8,128)(2,1)}, bf16[120,1,1440]{2,0,1:T(8,128)(2,1)}, u32[]{:S(2)}, u32[]{:S(2)}) collective-permute-start(bf16[120,1,1440]{2,0,1:T(8,128)(2,1)} %copy.22), channel_id=1, source_target_pairs={{1,0},{2,1},{3,2},{4,3},{5,4},{6,5},{7,6},{8,7},{9,8},{10,9},{11,1... | collective-permute-start | bytes 1036808 | tf_op jit(solution)/shard_map/ppermute | solution.py:19
  20.1 6.9 %copy-start.3 = (s32[120]{0:T(128)S(1)}, s32[120]{0:T(128)}, u32[]{:S(2)}) copy-start(s32[120]{0:T(128)} %param.7) | copy-start | bytes 1444
  26.1 5.1 %copy-start.1 = (bf16[120,8,1440]{2,1,0:T(8,128)(2,1)S(1)}, bf16[120,8,1440]{2,1,0:T(8,128)(2,1)}, u32[]{:S(2)}) copy-start(bf16[120,8,1440]{2,1,0:T(8,128)(2,1)} %param.4) | copy-start | bytes 8294404
  29.4 5.3 %slice-start = ((s8[5898240]{0:T(1024)(128)(4,1)}), s8[4194304]{0:T(1024)(128)(4,1)S(1)}, s32[]{:S(2)}) async-start(s8[5898240]{0:T(1024)(128)(4,1)} %bitcast.18), calls=%async_computation.1 | async-start | bytes 8388608
  31.2 3.5 slice-start.1
  31.2 3.5 copy-start.2
Sparse Core Ops, SparseCore 0:
  48.9 76.7 all-reduce.1
where the time goes:
time: 399 us; the launch traced here: 395 us
  blocking collectives  247 us (62%)
  waiting for transfers between devices  76.9 us (19%)
  local copies, waits for them, and re-layouts  23.6 us (6%)
  other arithmetic  17 us (4%)
  between operations  15 us (4%)
  matrix products  8.74 us (2%)
  starting transfers between devices  7.18 us (2%)
    psum x1, blocking collectives, local(): coeffs = lax.psum(projected, 'lat')  124 us
    psum x1, blocking collectives, local(): gram_sum = lax.psum(local_gram(sketch, cell_total), 'lat')  123 us
    psum x1, waiting for transfers between devices, local(): sketch = lax.psum(sketch, 'tm')  76.9 us
  transfers between devices with their start and end apart: 3, of which 1 were waited for; matrix products, arithmetic and copies ran while one was open for 2% of the time, Pallas kernels for 0%

commit v1 on v0

v1 whole, which is shorter than its diff:
```python
import functools

import jax
import jax.numpy as jnp
import numpy as np
from jax import lax
from jax.experimental import pallas as pl
from jax.experimental.pallas import tpu as pltpu
from jax.sharding import PartitionSpec as P

RANK = 32
LANE = 128
F32 = jnp.float32
BF16 = jnp.bfloat16
MESH = pl.DeviceIdType.MESH
HIGHEST = lax.Precision.HIGHEST
NSUB = 4
NLOAD = 5


def dot(a, b, precision=None):
    return lax.dot_general(
        a, b, (((1,), (0,)), ((), ())), precision=precision, preferred_element_type=F32
    )


def dot_t(a, b, precision=None):
    return lax.dot_general(
        a, b, (((1,), (1,)), ((), ())), precision=precision, preferred_element_type=F32
    )


def iota(shape, dim):
    return lax.broadcasted_iota(jnp.int32, shape, dim)


def split(x):
    high = x.astype(BF16)
    return high, (x - high.astype(F32)).astype(BF16)


def cosine(x):
    y = x * x
    p = jnp.full_like(y, -1.0 / 3628800.0)
    for coefficient in (1.0 / 40320.0, -1.0 / 720.0, 1.0 / 24.0, -0.5, 1.0):
        p = p * y + coefficient
    return p


def inverse_factor(gram):
    row, lane = iota((RANK, LANE), 0), iota((RANK, LANE), 1)
    a = jnp.where(lane == row + RANK, 1.0, gram)
    for k in range(RANK - 1):
        pivot_row = a[k : k + 1, :]
        column = a[:, k : k + 1]
        factor = column / a[k : k + 1, k : k + 1]
        a = a - jnp.where(row > k, factor * pivot_row, 0.0)
    diagonal = jnp.sum(jnp.where(row == lane, a, 0.0), axis=1, keepdims=True)
    scaled = a * lax.rsqrt(diagonal)
    return pltpu.roll(scaled, LANE - RANK, 1)[:, :RANK]


def kernel(
    shape,
    east_hbm,
    north_hbm,
    count_ref,
    ids_ref,
    basis_ref,
    coeffs_ref,
    east_raw,
    north_raw,
    east_f,
    north_f,
    edge_send,
    edge_recv,
    field,
    sketch,
    minus_send,
    minus_recv,
    plus_send,
    plus_recv,
    whole,
    grams,
    mine,
    pair_recv,
    x_slots,
    y_slots,
    load_sem,
    edge_ssem,
    edge_rsem,
    minus_ssem,
    minus_rsem,
    plus_ssem,
    plus_rsem,
    gm_ssem,
    gm_rsem,
    gp_ssem,
    gp_rsem,
    pair_sem,
    x_ssem,
    x_rsem,
    y_ssem,
    y_rsem,
):
    slots, rows, lons, n_tm, n_lat, n_x = shape
    n_y = n_lat // (2 * n_x)
    n_col = pl.cdiv(lons, LANE)
    tail = lons - (n_col - 1) * LANE
    padded = field.shape[1]
    width = n_col * LANE
    piece = width // NSUB
    total_rows = rows * n_lat
    cells = total_rows * lons

    m = lax.axis_index("tm")
    b = lax.axis_index("lat")
    core = lax.rem(b, 2)
    x = lax.rem(b // 2, n_x)
    y = b // (2 * n_x)
    z_plus, z_minus = {"tm": lax.rem(m + 1, n_tm)}, {"tm": lax.rem(m + n_tm - 1, n_tm)}
    south, north = {"lat": lax.rem(b + 1, n_lat)}, {"lat": lax.rem(b + n_lat - 1, n_lat)}
    partner = {"lat": b + 1 - 2 * core}

    def x_peer(d):
        return {"lat": (y * n_x + lax.rem(x + d, n_x)) * 2 + core}

    def y_peer(d):
        return {"lat": (lax.rem(y + d, n_y) * n_x + x) * 2 + core}

    peers = [z_plus, z_minus, south, north, partner]
    peers += [x_peer(d) for d in range(1, n_x)] + [y_peer(d) for d in range(1, n_y)]
    barrier = pltpu.get_barrier_semaphore()
    for peer in peers:
        pl.semaphore_signal(barrier, inc=1, device_id=peer, device_id_type=MESH)

    def remote(src, dst, ssem, rsem, peer):
        return pltpu.make_async_remote_copy(
            src_ref=src, dst_ref=dst, send_sem=ssem, recv_sem=rsem, device_id=peer, device_id_type=MESH
        )

    chunk = slots // NLOAD
    loads = []
    for which, (src, dst) in enumerate(((east_hbm, east_raw), (north_hbm, north_raw))):
        for i in range(NLOAD):
            part = pl.ds(i * chunk, chunk)
            copy = pltpu.make_async_copy(src.at[part], dst.at[part], load_sem.at[which, i])
            copy.start()
            loads.append(copy)

    ids = jnp.broadcast_to(ids_ref[...], (RANK, padded))
    column = iota((RANK, padded), 0)
    mixed = ids * 1103515245 + column * 40503 + 12345
    mixed = jnp.bitwise_xor(mixed, jnp.right_shift(mixed, 13))
    mixed = mixed * 1664525 + 1013904223
    mixed = jnp.bitwise_xor(mixed, jnp.right_shift(mixed, 16))
    flipped = jnp.bitwise_and(jnp.right_shift(mixed, 7), 1)
    slot_used = iota((RANK, padded), 1) < count_ref[0]
    signs = jnp.where(slot_used, (1 - 2 * flipped).astype(F32), 0.0).astype(BF16)

    band_row = iota((16, LANE), 0) + (b * rows - 1)
    cosines = cosine((total_rows // 2 - band_row).astype(F32) * (jnp.pi / 720.0))
    weights = 0.5 / jnp.sqrt(cosines)
    inside = jnp.logical_and(band_row >= 0, band_row < total_rows)
    cosines = jnp.where(inside, cosines, 0.0)

    zero_rows = padded * rows - slots * rows
    for store in (east_f, north_f):
        store[:, slots * rows :, :] = jnp.zeros((n_col, zero_rows, LANE), F32)
        store[n_col - 1] = jnp.zeros((padded * rows, LANE), F32)

    def widen(raw, store, copies):
        for i in range(NLOAD):
            copies[i].wait()
            for c in range(n_col):
                w = LANE if c < n_col - 1 else tail
                value = raw[i * chunk : (i + 1) * chunk, :, c * LANE : c * LANE + w]
                store[c, i * chunk * rows : (i + 1) * chunk * rows, 0:w] = value.astype(F32).reshape(
                    chunk * rows, w
                )

    widen(east_raw, east_f, loads[:NLOAD])
    for side, j in ((0, 0), (1, rows - 1)):
        for c in range(n_col):
            edge_send[side, :, c * LANE : (c + 1) * LANE] = east_f[c, pl.ds(j, padded, stride=rows), :].astype(
                BF16
            )
    pl.semaphore_wait(barrier, len(peers))
    edges = [
        remote(edge_send.at[0], edge_recv.at[1], edge_ssem.at[0], edge_rsem.at[1], north),
        remote(edge_send.at[1], edge_recv.at[0], edge_ssem.at[1], edge_rsem.at[0], south),
    ]
    for copy in edges:
        copy.start()
    widen(north_raw, north_f, loads[NLOAD:])

    lane16 = iota((16, LANE), 1)

    def field_row(j, east_above, east_below, c_above, c_below, weight):
        def group(g, carry):
            part = pl.ds(g * (16 * rows) + j, 16, stride=rows)
            w = [north_f[c, part, :] for c in range(n_col)]
            left = [pltpu.roll(t, LANE - 1, 1) for t in w]
            right = [pltpu.roll(t, 1, 1) for t in w]
            first_to_end = pltpu.roll(w[0], tail - 1, 1)
            end_to_first = pltpu.roll(w[-1], LANE - tail + 1, 1)
            for c in range(n_col):
                if c < n_col - 1:
                    nxt = jnp.where(lane16 < LANE - 1, left[c], left[c + 1])
                else:
                    nxt = jnp.where(lane16 < tail - 1, left[c], first_to_end)
                prv = jnp.where(lane16 > 0, right[c], right[c - 1] if c > 0 else end_to_first)
                value = (
                    (nxt - prv) - east_above(g, c) * c_above + east_below(g, c) * c_below
                ) * weight
                if c == n_col - 1:
                    value = jnp.where(lane16 < tail, value, 0.0)
                field[j, pl.ds(g * 16, 16), c * LANE : (c + 1) * LANE] = value.astype(BF16)
            return carry

        lax.fori_loop(0, padded // 16, group, 0)
        sketch[j] = dot(signs, field[j])

    def local_east(j):
        return lambda g, c: east_f[c, pl.ds(g * (16 * rows) + j, 16, stride=rows), :]

    def halo_east(side):
        return lambda g, c: edge_recv[side, pl.ds(g * 16, 16), c * LANE : (c + 1) * LANE].astype(F32)

    def table(t, i):
        return jnp.broadcast_to(t[i : i + 1, :], (16, LANE))

    for j in range(1, rows - 1):
        field_row(j, local_east(j - 1), local_east(j + 1), table(cosines, j), table(cosines, j + 2), table(weights, j + 1))
    edges[1].wait_recv()
    edges[0].wait_recv()
    j = 0
    field_row(j, halo_east(0), local_east(j + 1), table(cosines, j), table(cosines, j + 2), table(weights, j + 1))
    j = rows - 1
    field_row(j, local_east(j - 1), halo_east(1), table(cosines, j), table(cosines, j + 2), table(weights, j + 1))

    hops_minus, hops_plus = n_tm // 2, n_tm // 2 - 1

    def cols(h):
        return pl.ds(h * piece, piece)

    def chain(send, recv, ssem, rsem, peer, k, h):
        return remote(
            send.at[k, :, cols(h)], recv.at[k, :, cols(h)], ssem.at[k, h], rsem.at[k, h], peer
        )

    minus = functools.partial(chain, minus_send, minus_recv, minus_ssem, minus_rsem, z_minus)
    plus = functools.partial(chain, plus_send, plus_recv, plus_ssem, plus_rsem, z_plus)
    for k in range(hops_minus):
        for name, copy, send, recv, hops, j in (
            ("minus", minus, minus_send, minus_recv, hops_minus, lax.rem(m + hops_minus + k, n_tm)),
            ("plus", plus, plus_send, plus_recv, hops_plus, lax.rem(m + n_tm + hops_plus - k, n_tm)),
        ):
            if k >= hops:
                continue
            for h in range(NSUB):
                value = sketch[j, :, cols(h)]
                if k > 0:
                    copy(k - 1, h).wait_recv()
                    value = value + recv[k - 1, :, cols(h)].astype(F32)
                send[k, :, cols(h)] = value.astype(BF16)
                copy(k, h).start()

    def gather(ssem, rsem, peer, k, h, j):
        return remote(
            whole.at[j, :, cols(h)], whole.at[j, :, cols(h)], ssem.at[k, h], rsem.at[k, h], peer
        )

    to_minus = functools.partial(gather, gm_ssem, gm_rsem, z_minus)
    to_plus = functools.partial(gather, gp_ssem, gp_rsem, z_plus)
    for h in range(NSUB):
        plus(hops_plus - 1, h).wait_recv()
        minus(hops_minus - 1, h).wait_recv()
        value = sketch[m, :, cols(h)] + plus_recv[hops_plus - 1, :, cols(h)].astype(F32)
        value = value + minus_recv[hops_minus - 1, :, cols(h)].astype(F32)
        whole[m, :, cols(h)] = value.astype(BF16)
        to_minus(0, h, m).start()
        to_plus(0, h, m).start()

    mine[...] = jnp.zeros(mine.shape, F32)

    def consume(j):
        value = whole[j]
        mine[0:RANK, :] += dot_t(value, field[j])
        grams[j] = dot_t(value, value)

    consume(m)
    for k in range(1, hops_minus + 1):
        j_minus = lax.rem(m + k, n_tm)
        j_plus = lax.rem(m + n_tm - k, n_tm)
        for h in range(NSUB):
            to_minus(k - 1, h, j_minus).wait_recv()
            if k < hops_minus:
                to_minus(k, h, j_minus).start()
        if k <= hops_plus:
            for h in range(NSUB):
                to_plus(k - 1, h, j_plus).wait_recv()
                if k < hops_plus:
                    to_plus(k, h, j_plus).start()
        consume(j_minus)
        if k <= hops_plus:
            consume(j_plus)

    gram = grams[0]
    for j in range(1, rows):
        gram = gram + grams[j]
    mine[RANK : 2 * RANK, 0:RANK] = gram

    pair = remote(mine, pair_recv, pair_sem.at[0], pair_sem.at[1], partner)
    pair.start()
    pair.wait_recv()
    value = mine[...] + pair_recv[...]
    for store, ssem, rsem, count, here, peer_of in (
        (x_slots, x_ssem, x_rsem, n_x, x, x_peer),
        (y_slots, y_ssem, y_rsem, n_y, y, y_peer),
    ):
        store[here] = value
        for d in range(1, count):
            remote(store.at[here], store.at[here], ssem.at[d - 1], rsem.at[d - 1], peer_of(d)).start()
        for d in range(1, count):
            origin = lax.rem(here + count - d, count)
            remote(store.at[origin], store.at[origin], ssem.at[d - 1], rsem.at[d - 1], peer_of(d)).wait_recv()
        value = store[0]
        for i in range(1, count):
            value = value + store[i]

    projected = value[0:RANK, :]
    inverse = inverse_factor(value[RANK : 2 * RANK, :] * (1.0 / cells))
    coeffs = dot(inverse, projected, HIGHEST) * (1.0 / cells)
    coeffs = jnp.where(iota((RANK, padded), 1) < count_ref[0], coeffs, 0.0)
    coeffs_ref[...] = coeffs[:, :slots]

    size = RANK * rows
    take_row = (iota((size, RANK), 0) // rows == iota((size, RANK), 1)).astype(F32).astype(BF16)
    take_col = (iota((RANK, size), 0) == lax.rem(iota((RANK, size), 1), RANK)).astype(F32).astype(BF16)
    same = lax.rem(iota((size, size), 0), rows) == iota((size, size), 1) // RANK
    flat = whole[...].reshape(size, width)
    basis = None
    for half in split(inverse):
        spread = dot(take_row, half).astype(BF16)
        spread = dot(spread, take_col)
        spread = jnp.where(same, spread, 0.0).astype(BF16)
        term = dot(spread, flat)
        basis = term if basis is None else basis + term
    basis_ref[...] = basis.reshape(RANK, rows, width)[:, :, :lons].astype(BF16)

    for copy in edges:
        copy.wait_send()
    for h in range(NSUB):
        for k in range(hops_minus):
            minus(k, h).wait_send()
            to_minus(k, h, m).wait_send()
        for k in range(hops_plus):
            plus(k, h).wait_send()
            to_plus(k, h, m).wait_send()
    pair.wait_send()
    for store, ssem, rsem, count, here, peer_of in (
        (x_slots, x_ssem, x_rsem, n_x, x, x_peer),
        (y_slots, y_ssem, y_rsem, n_y, y, y_peer),
    ):
        for d in range(1, count):
            remote(store.at[here], store.at[here], ssem.at[d - 1], rsem.at[d - 1], peer_of(d)).wait_send()


def local(n_tm, n_lat, n_x, wind_east, wind_north, snap_counts, snap_ids):
    slots, rows, lons = wind_east.shape
    padded = -(-slots // LANE) * LANE
    n_col = -(-lons // LANE)
    width = n_col * LANE
    n_y = n_lat // (2 * n_x)
    ids = jnp.pad(snap_ids, (0, padded - slots)).reshape(1, padded)
    shape = (slots, rows, lons, n_tm, n_lat, n_x)
    hm, hp = n_tm // 2, n_tm // 2 - 1
    dma = pltpu.SemaphoreType.DMA
    return pl.pallas_call(
        functools.partial(kernel, shape),
        out_shape=(
            jax.ShapeDtypeStruct((RANK, rows, lons), BF16),
            jax.ShapeDtypeStruct((RANK, slots), F32),
        ),
        in_specs=[
            pl.BlockSpec(memory_space=pl.ANY),
            pl.BlockSpec(memory_space=pl.ANY),
            pl.BlockSpec(memory_space=pltpu.SMEM),
            pl.BlockSpec(memory_space=pltpu.VMEM),
        ],
        out_specs=(pl.BlockSpec(memory_space=pltpu.VMEM), pl.BlockSpec(memory_space=pltpu.VMEM)),
        scratch_shapes=[
            pltpu.VMEM((slots, rows, lons), BF16),
            pltpu.VMEM((slots, rows, lons), BF16),
            pltpu.VMEM((n_col, padded * rows, LANE), F32),
            pltpu.VMEM((n_col, padded * rows, LANE), F32),
            pltpu.VMEM((2, padded, width), BF16),
            pltpu.VMEM((2, padded, width), BF16),
            pltpu.VMEM((rows, padded, width), BF16),
            pltpu.VMEM((rows, RANK, width), F32),
            pltpu.VMEM((hm, RANK, width), BF16),
            pltpu.VMEM((hm, RANK, width), BF16),
            pltpu.VMEM((hp, RANK, width), BF16),
            pltpu.VMEM((hp, RANK, width), BF16),
            pltpu.VMEM((rows, RANK, width), BF16),
            pltpu.VMEM((rows, RANK, RANK), F32),
            pltpu.VMEM((2 * RANK, LANE), F32),
            pltpu.VMEM((2 * RANK, LANE), F32),
            pltpu.VMEM((n_x, 2 * RANK, LANE), F32),
            pltpu.VMEM((n_y, 2 * RANK, LANE), F32),
            dma((2, NLOAD)),
            dma((2,)),
            dma((2,)),
            dma((hm, NSUB)),
            dma((hm, NSUB)),
            dma((hp, NSUB)),
            dma((hp, NSUB)),
            dma((hm, NSUB)),
            dma((hm, NSUB)),
            dma((hp, NSUB)),
            dma((hp, NSUB)),
            dma((2,)),
            dma((n_x - 1,)),
            dma((n_x - 1,)),
            dma((n_y - 1,)),
            dma((n_y - 1,)),
        ],
        compiler_params=pltpu.CompilerParams(
            collective_id=0, has_side_effects=True, vmem_limit_bytes=60 * 1024 * 1024
        ),
        name="eof",
    )(wind_east, wind_north, snap_counts, ids)


def solution(mesh):
    in_specs = (P("tm", "lat", None), P("tm", "lat", None), P("tm"), P("tm"))
    out_specs = (P(None, "lat", None), P(None, "tm"))
    body = functools.partial(local, mesh.shape["tm"], mesh.shape["lat"], 4)
    return jax.shard_map(body, mesh=mesh, in_specs=in_specs, out_specs=out_specs, check_vma=False)
```

time: 399 us -> 67.1 us (0.17)
  blocking collectives: 247 us -> 0 us
  waiting for transfers between devices: 76.9 us -> 0 us
  Pallas kernels: 0 us -> 61.1 us
  local copies, waits for them, and re-layouts: 23.6 us -> 4.55 us
  other arithmetic: 17 us -> 0 us
  between operations: 15 us -> 1.29 us
  matrix products: 8.74 us -> 0 us
  starting transfers between devices: 7.18 us -> 0 us
    psum x2 -> x0, blocking collectives: 247 us -> none  [the longest x1 124 us: local(): coeffs = lax.psum(projected, 'lat')]
    psum x1 -> x0, waiting for transfers between devices: 76.9 us -> none  [local(): sketch = lax.psum(sketch, 'tm')]
    pallas_call x0 -> x1, Pallas kernels: none -> 61.1 us  [local(): pl.pallas_call(functools.partial(kernel, shape), out_shape=(jax.ShapeDtyp...]
    slice x3 -> x0, local copies, waits for them, and re-layouts: 10.9 us -> none  [the longest x2 6.85 us: metric_vorticity(): jnp.roll(meridional, 1, axis=2)]
    dot_general x4 -> x0, matrix products: 8.52 us -> none  [the longest x1 3.17 us: local_gram(): lax.dot_general(sketch, sketch, (((1,), (1,)), ((), ())), precision=lax.P...]
    ppermute x2 -> x0, starting transfers between devices: 7.14 us -> none  [the longest x1 4.49 us: with_halo(): lax.ppermute(tail, axis, [(i, (i + 1) % count) for i in range(ends)])]
    another operation x5 -> x0, other arithmetic: 6.68 us -> none  [the longest x3 3.59 us: orthonormal(): factor = jnp.linalg.cholesky(gram_sum)]
    convert_element_type x2 -> x0, other arithmetic: 6.67 us -> none  [the longest x1 6.66 us: metric_vorticity(): return field.astype(jnp.bfloat16)]
  transfers between devices with their start and end apart: 3 -> 0, of which waited for: 1 -> 0; matrix products, arithmetic and copies ran while one was open for 2% -> 0% of each run, Pallas kernels for 0% -> 0%
where the time goes in v1:
time: 67.1 us; the launch traced here: 66.9 us
  Pallas kernels  61.1 us (91%)
  local copies, waits for them, and re-layouts  4.55 us (7%)
  between operations  1.29 us (2%)
    pallas_call x1, Pallas kernels, local(): pl.pallas_call(functools.partial(kernel, shape), out_shape=(jax.ShapeDtyp...  61.1 us
    unnamed x2, local copies, waits for them, and re-layouts  3.39 us

profile of v1, /device:TPU:1, one launch (start us, length us, event | category | flops | bytes accessed | tf_op | source)
XLA Modules:
  0.0 66.9 jit_solution(7403681130537159882)
XLA Ops:
  1.3 1.2 %pad_bitcast_fusion.ids_ref = s32[1,128]{1,0:T(1,128)} fusion(s32[120]{0:T(128)} %param.7), kind=kLoop, calls=%fused_computation | loop fusion | bytes 992 | tf_op jit(solution)/shard_map/reshape | solution.py:376
  2.4 61.1 %eof.1 = (bf16[32,8,1440]{2,1,0:T(8,128)(2,1)}, f32[32,120]{1,0:T(8,128)}) custom-call(bf16[120,8,1440]{2,1,0:T(8,128)(2,1)} %east_hbm.1, bf16[120,8,1440]{2,1,0:T(8,128)(2,1)} %north_hbm.1, s32[1]{0:T(128)S(6)} %copy.8.count_ref, s32[1,128]{1,0:T(1,128)} %pad_bitcast_fusion.ids_ref), custom_call_target="tpu_custom_call" | custom-call | tf_op jit(solution)/shard_map/eof/pallas_call | solution.py:380
  63.5 2.1 %copy.9 = bf16[32,8,1440]{2,1,0:T(8,128)(2,1)} copy(bf16[32,8,1440]{2,1,0:T(8,128)(2,1)} %get-tuple-element.4) | data formatting | bytes 1474560
  65.6 1.3 %copy.10 = f32[32,120]{1,0:T(8,128)} copy(f32[32,120]{1,0:T(8,128)} %get-tuple-element.5) | data formatting | bytes 30720

commit v2 on v1

--- a/solution.py
+++ b/solution.py
@@ -76,10 +76,9 @@
     edge_recv,
     field,
     sketch,
-    minus_send,
-    minus_recv,
-    plus_send,
-    plus_recv,
+    tables,
+    chain_send,
+    chain_recv,
     whole,
     grams,
     mine,
@@ -89,14 +88,10 @@
     load_sem,
     edge_ssem,
     edge_rsem,
-    minus_ssem,
-    minus_rsem,
-    plus_ssem,
-    plus_rsem,
-    gm_ssem,
-    gm_rsem,
-    gp_ssem,
-    gp_rsem,
+    chain_ssem,
+    chain_rsem,
+    gather_ssem,
+    gather_rsem,
     pair_sem,
     x_ssem,
     x_rsem,
@@ -162,12 +157,13 @@
     cosines = cosine((total_rows // 2 - band_row).astype(F32) * (jnp.pi / 720.0))
     weights = 0.5 / jnp.sqrt(cosines)
     inside = jnp.logical_and(band_row >= 0, band_row < total_rows)
-    cosines = jnp.where(inside, cosines, 0.0)
+    tables[0] = jnp.where(inside, cosines, 0.0)
+    tables[1] = weights
 
     zero_rows = padded * rows - slots * rows
     for store in (east_f, north_f):
-        store[:, slots * rows :, :] = jnp.zeros((n_col, zero_rows, LANE), F32)
-        store[n_col - 1] = jnp.zeros((padded * rows, LANE), F32)
+        store[:, slots * rows : padded * rows, :] = jnp.zeros((n_col, zero_rows, LANE), F32)
+        store[n_col - 1, 0 : padded * rows, :] = jnp.zeros((padded * rows, LANE), F32)
 
     def widen(raw, store, copies):
         for i in range(NLOAD):
@@ -185,6 +181,8 @@
             edge_send[side, :, c * LANE : (c + 1) * LANE] = east_f[c, pl.ds(j, padded, stride=rows), :].astype(
                 BF16
             )
+    widen(north_raw, north_f, loads[NLOAD:])
+
     pl.semaphore_wait(barrier, len(peers))
     edges = [
         remote(edge_send.at[0], edge_recv.at[1], edge_ssem.at[0], edge_rsem.at[1], north),
@@ -192,14 +190,23 @@
     ]
     for copy in edges:
         copy.start()
-    widen(north_raw, north_f, loads[NLOAD:])
 
     lane16 = iota((16, LANE), 1)
 
-    def field_row(j, east_above, east_below, c_above, c_below, weight):
+    def compute_row(j):
+        above = jnp.where(j > 0, j - 1, padded * rows)
+        below = jnp.where(j < rows - 1, j + 1, padded * rows + 1)
+
+        def table(t, i):
+            return jnp.broadcast_to(tables[t, pl.ds(i, 1), :], (16, LANE))
+
+        c_above, c_below, weight = table(0, j), table(0, j + 2), table(1, j + 1)
+
         def group(g, carry):
-            part = pl.ds(g * (16 * rows) + j, 16, stride=rows)
-            w = [north_f[c, part, :] for c in range(n_col)]
+            def part(first):
+                return pl.ds(g * (16 * rows) + first, 16, stride=rows)
+
+            w = [north_f[c, part(j), :] for c in range(n_col)]
             left = [pltpu.roll(t, LANE - 1, 1) for t in w]
             right = [pltpu.roll(t, 1, 1) for t in w]
             first_to_end = pltpu.roll(w[0], tail - 1, 1)
@@ -211,7 +218,7 @@
                     nxt = jnp.where(lane16 < tail - 1, left[c], first_to_end)
                 prv = jnp.where(lane16 > 0, right[c], right[c - 1] if c > 0 else end_to_first)
                 value = (
-                    (nxt - prv) - east_above(g, c) * c_above + east_below(g, c) * c_below
+                    (nxt - prv) - east_f[c, part(above), :] * c_above + east_f[c, part(below), :] * c_below
                 ) * weight
                 if c == n_col - 1:
                     value = jnp.where(lane16 < tail, value, 0.0)
@@ -221,90 +228,151 @@
         lax.fori_loop(0, padded // 16, group, 0)
         sketch[j] = dot(signs, field[j])
 
-    def local_east(j):
-        return lambda g, c: east_f[c, pl.ds(g * (16 * rows) + j, 16, stride=rows), :]
-
-    def halo_east(side):
-        return lambda g, c: edge_recv[side, pl.ds(g * 16, 16), c * LANE : (c + 1) * LANE].astype(F32)
-
-    def table(t, i):
-        return jnp.broadcast_to(t[i : i + 1, :], (16, LANE))
-
-    for j in range(1, rows - 1):
-        field_row(j, local_east(j - 1), local_east(j + 1), table(cosines, j), table(cosines, j + 2), table(weights, j + 1))
-    edges[1].wait_recv()
-    edges[0].wait_recv()
-    j = 0
-    field_row(j, halo_east(0), local_east(j + 1), table(cosines, j), table(cosines, j + 2), table(weights, j + 1))
-    j = rows - 1
-    field_row(j, local_east(j - 1), halo_east(1), table(cosines, j), table(cosines, j + 2), table(weights, j + 1))
-
-    hops_minus, hops_plus = n_tm // 2, n_tm // 2 - 1
+    def take_halo():
+        for side in (0, 1):
+            edges[1 - side].wait_recv()
+            for c in range(n_col):
+                east_f[c, pl.ds(padded * rows + side, padded, stride=rows), :] = edge_recv[
+                    side, :, c * LANE : (c + 1) * LANE
+                ].astype(F32)
+
+    hops = n_tm // 2
+    halves = (range(0, NSUB // 2), range(NSUB // 2, NSUB))
 
     def cols(h):
         return pl.ds(h * piece, piece)
 
-    def chain(send, recv, ssem, rsem, peer, k, h):
+    def row_at(offset):
+        return lax.rem(m + n_tm + offset, n_tm)
+
+    def when_class(j, edge, run):
+        is_edge = jnp.logical_or(j == 0, j == rows - 1)
+        pl.when(is_edge if edge else jnp.logical_not(is_edge))(run)
+
+    def chain(side, k, h):
         return remote(
-            send.at[k, :, cols(h)], recv.at[k, :, cols(h)], ssem.at[k, h], rsem.at[k, h], peer
+            chain_send.at[side, k, :, cols(h)],
+            chain_recv.at[side, k, :, cols(h)],
+            chain_ssem.at[side, k, h],
+            chain_rsem.at[side, k, h],
+            (z_minus, z_plus)[side],
         )
 
-    minus = functools.partial(chain, minus_send, minus_recv, minus_ssem, minus_rsem, z_minus)
-    plus = functools.partial(chain, plus_send, plus_recv, plus_ssem, plus_rsem, z_plus)
-    for k in range(hops_minus):
-        for name, copy, send, recv, hops, j in (
-            ("minus", minus, minus_send, minus_recv, hops_minus, lax.rem(m + hops_minus + k, n_tm)),
-            ("plus", plus, plus_send, plus_recv, hops_plus, lax.rem(m + n_tm + hops_plus - k, n_tm)),
-        ):
-            if k >= hops:
-                continue
-            for h in range(NSUB):
-                value = sketch[j, :, cols(h)]
-                if k > 0:
-                    copy(k - 1, h).wait_recv()
-                    value = value + recv[k - 1, :, cols(h)].astype(F32)
-                send[k, :, cols(h)] = value.astype(BF16)
-                copy(k, h).start()
-
-    def gather(ssem, rsem, peer, k, h, j):
+    def chain_row(side, k):
+        return row_at(hops + k) if side == 0 else row_at(hops - k)
+
+    def begin(k, edge):
+        for side in (0, 1):
+            j = chain_row(side, k)
+
+            def run(side=side, j=j):
+                compute_row(j)
+                if k > 1:
+                    return
+                for other in (0, 1):
+                    if k == 1 and other == side:
+                        continue
+                    for h in halves[other]:
+                        target = side if k == 1 else other
+                        chain_send[target, k, :, cols(h)] = sketch[j, :, cols(h)].astype(BF16)
+                        chain(target, k, h).start()
+
+            if k > 0 or side == 0:
+                when_class(j, edge, run)
+
+    def relay(k, edge):
+        for side in (0, 1):
+            j = chain_row(side, k)
+
+            def run(side=side, j=j):
+                for h in halves[side] if k == 1 else range(NSUB):
+                    chain(side, k - 1, h).wait_recv()
+                    value = sketch[j, :, cols(h)] + chain_recv[side, k - 1, :, cols(h)].astype(F32)
+                    chain_send[side, k, :, cols(h)] = value.astype(BF16)
+                    chain(side, k, h).start()
+
+            when_class(j, edge, run)
+
+    def gather(side, k, h, j):
         return remote(
-            whole.at[j, :, cols(h)], whole.at[j, :, cols(h)], ssem.at[k, h], rsem.at[k, h], peer
+            whole.at[j, :, cols(h)],
+            whole.at[j, :, cols(h)],
+            gather_ssem.at[side, k, h],
+            gather_rsem.at[side, k, h],
+            (z_minus, z_plus)[side],
         )
-
-    to_minus = functools.partial(gather, gm_ssem, gm_rsem, z_minus)
-    to_plus = functools.partial(gather, gp_ssem, gp_rsem, z_plus)
-    for h in range(NSUB):
-        plus(hops_plus - 1, h).wait_recv()
-        minus(hops_minus - 1, h).wait_recv()
-        value = sketch[m, :, cols(h)] + plus_recv[hops_plus - 1, :, cols(h)].astype(F32)
-        value = value + minus_recv[hops_minus - 1, :, cols(h)].astype(F32)
-        whole[m, :, cols(h)] = value.astype(BF16)
-        to_minus(0, h, m).start()
-        to_plus(0, h, m).start()
-
-    mine[...] = jnp.zeros(mine.shape, F32)
 
     def consume(j):
         value = whole[j]
         mine[0:RANK, :] += dot_t(value, field[j])
         grams[j] = dot_t(value, value)
 
-    consume(m)
-    for k in range(1, hops_minus + 1):
-        j_minus = lax.rem(m + k, n_tm)
-        j_plus = lax.rem(m + n_tm - k, n_tm)
-        for h in range(NSUB):
-            to_minus(k - 1, h, j_minus).wait_recv()
-            if k < hops_minus:
-                to_minus(k, h, j_minus).start()
-        if k <= hops_plus:
+    def finish(edge):
+        def run():
             for h in range(NSUB):
-                to_plus(k - 1, h, j_plus).wait_recv()
-                if k < hops_plus:
-                    to_plus(k, h, j_plus).start()
-        consume(j_minus)
-        if k <= hops_plus:
-            consume(j_plus)
+                value = sketch[m, :, cols(h)]
+                for side in (0, 1):
+                    chain(side, hops - 1, h).wait_recv()
+                    value = value + chain_recv[side, hops - 1, :, cols(h)].astype(F32)
+                whole[m, :, cols(h)] = value.astype(BF16)
+                for side in (0, 1):
+                    gather(side, 0, h, m).start()
+            consume(m)
+
+        when_class(m, edge, run)
+
+    def spread(k, edge):
+        for side in (0, 1):
+            j = row_at(k) if side == 0 else row_at(-k)
+
+            def run(side=side, j=j):
+                for h in range(NSUB):
+                    gather(side, k - 1, h, j).wait_recv()
+                    if k < hops - 1 or h in halves[side]:
+                        gather(side, k, h, j).start()
+                consume(j)
+
+            when_class(j, edge, run)
+
+    def last(edge):
+        j = row_at(hops)
+
+        def run():
+            for side in (0, 1):
+                for h in halves[side]:
+                    gather(side, hops - 1, h, j).wait_recv()
+            consume(j)
+
+        when_class(j, edge, run)
+
+    mine[...] = jnp.zeros(mine.shape, F32)
+    begin(0, False)
+    begin(1, False)
+    relay(1, False)
+    take_halo()
+    begin(0, True)
+    begin(2, False)
+    begin(1, True)
+    relay(2, False)
+    relay(1, True)
+    begin(3, False)
+    begin(2, True)
+    relay(3, False)
+    relay(2, True)
+    begin(3, True)
+    compute_row(m)
+    relay(3, True)
+    finish(False)
+    finish(True)
+    for k in range(1, hops + 1):
+        if k < hops:
+            spread(k, False)
+        else:
+            last(False)
+        if k == 1:
+            continue
+        spread(k - 1, True)
+    last(True)
 
     gram = grams[0]
     for j in range(1, rows):
@@ -351,13 +419,13 @@
 
     for copy in edges:
         copy.wait_send()
-    for h in range(NSUB):
-        for k in range(hops_minus):
-            minus(k, h).wait_send()
-            to_minus(k, h, m).wait_send()
-        for k in range(hops_plus):
-            plus(k, h).wait_send()
-            to_plus(k, h, m).wait_send()
+    for side in (0, 1):
+        for k in range(hops):
+            for h in range(NSUB):
+                if k > 0 or h in halves[side]:
+                    chain(side, k, h).wait_send()
+                if k < hops - 1 or h in halves[side]:
+                    gather(side, k, h, m).wait_send()
     pair.wait_send()
     for store, ssem, rsem, count, here, peer_of in (
         (x_slots, x_ssem, x_rsem, n_x, x, x_peer),
@@ -375,7 +443,7 @@
     n_y = n_lat // (2 * n_x)
     ids = jnp.pad(snap_ids, (0, padded - slots)).reshape(1, padded)
     shape = (slots, rows, lons, n_tm, n_lat, n_x)
-    hm, hp = n_tm // 2, n_tm // 2 - 1
+    hops = n_tm // 2
     dma = pltpu.SemaphoreType.DMA
     return pl.pallas_call(
         functools.partial(kernel, shape),
@@ -393,16 +461,15 @@
         scratch_shapes=[
             pltpu.VMEM((slots, rows, lons), BF16),
             pltpu.VMEM((slots, rows, lons), BF16),
-            pltpu.VMEM((n_col, padded * rows, LANE), F32),
+            pltpu.VMEM((n_col, 2 * padded * rows, LANE), F32),
             pltpu.VMEM((n_col, padded * rows, LANE), F32),
             pltpu.VMEM((2, padded, width), BF16),
             pltpu.VMEM((2, padded, width), BF16),
             pltpu.VMEM((rows, padded, width), BF16),
             pltpu.VMEM((rows, RANK, width), F32),
-            pltpu.VMEM((hm, RANK, width), BF16),
-            pltpu.VMEM((hm, RANK, width), BF16),
-            pltpu.VMEM((hp, RANK, width), BF16),
-            pltpu.VMEM((hp, RANK, width), BF16),
+            pltpu.VMEM((2, 16, LANE), F32),
+            pltpu.VMEM((2, hops, RANK, width), BF16),
+            pltpu.VMEM((2, hops, RANK, width), BF16),
             pltpu.VMEM((rows, RANK, width), BF16),
             pltpu.VMEM((rows, RANK, RANK), F32),
             pltpu.VMEM((2 * RANK, LANE), F32),
@@ -412,14 +479,10 @@
             dma((2, NLOAD)),
             dma((2,)),
             dma((2,)),
-            dma((hm, NSUB)),
-            dma((hm, NSUB)),
-            dma((hp, NSUB)),
-            dma((hp, NSUB)),
-            dma((hm, NSUB)),
-            dma((hm, NSUB)),
-            dma((hp, NSUB)),
-            dma((hp, NSUB)),
+            dma((2, hops, NSUB)),
+            dma((2, hops, NSUB)),
+            dma((2, hops, NSUB)),
+            dma((2, hops, NSUB)),
             dma((2,)),
             dma((n_x - 1,)),
             dma((n_x - 1,)),

time: 67.1 us -> 69.4 us (1.034)
  Pallas kernels: 61.1 us -> 62.9 us
    pallas_call x1, Pallas kernels: 61.1 us -> 62.9 us  [local(): pl.pallas_call(functools.partial(kernel, shape), out_shape=(jax.ShapeDtyp...]
where the time goes in v2:
time: 69.4 us; the launch traced here: 68.7 us
  Pallas kernels  62.9 us (91%)
  local copies, waits for them, and re-layouts  4.55 us (7%)
  between operations  1.29 us (2%)
    pallas_call x1, Pallas kernels, local(): pl.pallas_call(functools.partial(kernel, shape), out_shape=(jax.ShapeDtyp...  62.9 us
    unnamed x2, local copies, waits for them, and re-layouts  3.39 us

profile of v2, /device:TPU:1, one launch (start us, length us, event | category | flops | bytes accessed | tf_op | source)
XLA Modules:
  0.0 68.7 jit_solution(15932510089789793398)
XLA Ops:
  1.3 1.2 %pad_bitcast_fusion.ids_ref = s32[1,128]{1,0:T(1,128)} fusion(s32[120]{0:T(128)} %param.7), kind=kLoop, calls=%fused_computation | loop fusion | bytes 992 | tf_op jit(solution)/shard_map/reshape | solution.py:444
  2.4 62.9 %eof.1 = (bf16[32,8,1440]{2,1,0:T(8,128)(2,1)}, f32[32,120]{1,0:T(8,128)}) custom-call(bf16[120,8,1440]{2,1,0:T(8,128)(2,1)} %east_hbm.1, bf16[120,8,1440]{2,1,0:T(8,128)(2,1)} %north_hbm.1, s32[1]{0:T(128)S(6)} %copy.8.count_ref, s32[1,128]{1,0:T(1,128)} %pad_bitcast_fusion.ids_ref), custom_call_target="tpu_custom_call" | custom-call | tf_op jit(solution)/shard_map/eof/pallas_call | solution.py:448
  65.3 2.1 %copy.9 = bf16[32,8,1440]{2,1,0:T(8,128)(2,1)} copy(bf16[32,8,1440]{2,1,0:T(8,128)(2,1)} %get-tuple-element.4) | data formatting | bytes 1474560
  67.4 1.3 %copy.10 = f32[32,120]{1,0:T(8,128)} copy(f32[32,120]{1,0:T(8,128)} %get-tuple-element.5) | data formatting | bytes 30720

commit v3 on v1

v3 whole, which is shorter than its diff:
```python
import functools

import jax
import jax.numpy as jnp
import numpy as np
from jax import lax
from jax.experimental import pallas as pl
from jax.experimental.pallas import tpu as pltpu
from jax.sharding import PartitionSpec as P

RANK = 32
LANE = 128
F32 = jnp.float32
BF16 = jnp.bfloat16
MESH = pl.DeviceIdType.MESH
HIGHEST = lax.Precision.HIGHEST
NSUB = 4


def dot(a, b, precision=None):
    return lax.dot_general(
        a, b, (((1,), (0,)), ((), ())), precision=precision, preferred_element_type=F32
    )


def dot_t(a, b, precision=None):
    return lax.dot_general(
        a, b, (((1,), (1,)), ((), ())), precision=precision, preferred_element_type=F32
    )


def iota(shape, dim):
    return lax.broadcasted_iota(jnp.int32, shape, dim)


def split(x):
    high = x.astype(BF16)
    return high, (x - high.astype(F32)).astype(BF16)


def cosine(x):
    y = x * x
    p = jnp.full_like(y, -1.0 / 3628800.0)
    for coefficient in (1.0 / 40320.0, -1.0 / 720.0, 1.0 / 24.0, -0.5, 1.0):
        p = p * y + coefficient
    return p


def inverse_factor(gram):
    row, lane = iota((RANK, LANE), 0), iota((RANK, LANE), 1)
    a = jnp.where(lane == row + RANK, 1.0, gram)
    for k in range(RANK - 1):
        pivot_row = a[k : k + 1, :]
        column = a[:, k : k + 1]
        factor = column / a[k : k + 1, k : k + 1]
        a = a - jnp.where(row > k, factor * pivot_row, 0.0)
    diagonal = jnp.sum(jnp.where(row == lane, a, 0.0), axis=1, keepdims=True)
    scaled = a * lax.rsqrt(diagonal)
    return pltpu.roll(scaled, LANE - RANK, 1)[:, :RANK]


def kernel(
    shape,
    east_hbm,
    north_hbm,
    count_ref,
    ids_ref,
    basis_ref,
    coeffs_ref,
    east_f,
    north_f,
    east_b,
    north_b,
    spread_signs,
    east_sketch,
    north_sketch,
    sketch,
    halo_send,
    halo_recv,
    edge_send,
    edge_recv,
    field,
    chain_send,
    chain_recv,
    whole,
    projection,
    gram_part,
    gram_slots,
    x_slots,
    y_slots,
    load_sem,
    halo_ssem,
    halo_rsem,
    edge_ssem,
    edge_rsem,
    chain_ssem,
    chain_rsem,
    gather_ssem,
    gather_rsem,
    gram_ssem,
    gram_rsem,
    x_ssem,
    x_rsem,
    y_ssem,
    y_rsem,
):
    slots, rows, lons, n_tm, n_lat, n_x = shape
    n_y = n_lat // (2 * n_x)
    n_col = pl.cdiv(lons, LANE)
    tail = lons - (n_col - 1) * LANE
    padded = field.shape[1]
    width = n_col * LANE
    piece = width // NSUB
    total_rows = rows * n_lat
    cells = total_rows * lons

    m = lax.axis_index("tm")
    b = lax.axis_index("lat")
    core = lax.rem(b, 2)
    x = lax.rem(b // 2, n_x)
    y = b // (2 * n_x)
    south, north = {"lat": lax.rem(b + 1, n_lat)}, {"lat": lax.rem(b + n_lat - 1, n_lat)}

    def z_at(d):
        return {"tm": lax.rem(m + n_tm + d, n_tm)}

    def x_peer(i, sign=1):
        dx, flip = i // 2, i % 2
        other = core + flip - 2 * flip * core
        return lax.rem(x + n_x + sign * dx, n_x) * 2 + other

    def y_peer(d, sign=1):
        return lax.rem(y + n_y + sign * d, n_y)

    x_line = [{"lat": y * (2 * n_x) + x_peer(i)} for i in range(1, 2 * n_x)]
    y_line = [{"lat": y_peer(d) * (2 * n_x) + x * 2 + core} for d in range(1, n_y)]
    peers = [z_at(d) for d in (-2, -1, 1, 2)] + [south, north] + x_line + y_line
    barrier = pltpu.get_barrier_semaphore()
    for peer in peers:
        pl.semaphore_signal(barrier, inc=1, device_id=peer, device_id_type=MESH)

    def remote(src, dst, ssem, rsem, peer):
        return pltpu.make_async_remote_copy(
            src_ref=src, dst_ref=dst, send_sem=ssem, recv_sem=rsem, device_id=peer, device_id_type=MESH
        )

    loads = [
        pltpu.make_async_copy(east_hbm, east_b, load_sem.at[0]),
        pltpu.make_async_copy(north_hbm, north_b, load_sem.at[1]),
    ]
    for copy in loads:
        copy.start()

    ids = jnp.broadcast_to(ids_ref[...], (RANK, slots))
    column = iota((RANK, slots), 0)
    mixed = ids * 1103515245 + column * 40503 + 12345
    mixed = jnp.bitwise_xor(mixed, jnp.right_shift(mixed, 13))
    mixed = mixed * 1664525 + 1013904223
    mixed = jnp.bitwise_xor(mixed, jnp.right_shift(mixed, 16))
    flipped = jnp.bitwise_and(jnp.right_shift(mixed, 7), 1)
    slot_used = iota((RANK, slots), 1) < count_ref[0]
    signs = jnp.where(slot_used, (1 - 2 * flipped).astype(F32), 0.0).astype(BF16)
    depth = slots * rows
    repeat = (iota((slots, depth), 1) // rows == iota((slots, depth), 0)).astype(F32).astype(BF16)
    repeated = dot(signs, repeat)
    lane_row = lax.rem(iota((RANK, depth), 1), rows)
    for j in range(rows):
        spread_signs[j * RANK : (j + 1) * RANK, :] = jnp.where(lane_row == j, repeated, 0.0).astype(BF16)

    band_row = iota((16, LANE), 0) + (b * rows - 1)
    cosines = cosine((total_rows // 2 - band_row).astype(F32) * (jnp.pi / 720.0))
    weights = 0.5 / jnp.sqrt(cosines)
    inside = jnp.logical_and(band_row >= 0, band_row < total_rows)
    cosines = jnp.where(inside, cosines, 0.0)

    for wide in (east_f, north_f):
        wide[:, depth:, :] = jnp.zeros((n_col, padded * rows - depth, LANE), F32)

    loads[0].wait()
    east_sketch[1 : rows + 1, :, 0:lons] = dot(spread_signs[...], east_b[...]).reshape(rows, RANK, lons)
    for side, j in ((0, 1), (1, rows)):
        halo_send[side] = east_sketch[j].astype(BF16)
    pl.semaphore_wait(barrier, len(peers))
    halos = [
        remote(halo_send.at[0], halo_recv.at[1], halo_ssem.at[0], halo_rsem.at[1], north),
        remote(halo_send.at[1], halo_recv.at[0], halo_ssem.at[1], halo_rsem.at[0], south),
    ]
    for copy in halos:
        copy.start()
    loads[1].wait()
    north_sketch[:, :, 0:lons] = dot(spread_signs[...], north_b[...]).reshape(rows, RANK, lons)

    def roll_pair(tiles, lane):
        left = [pltpu.roll(t, LANE - 1, 1) for t in tiles]
        right = [pltpu.roll(t, 1, 1) for t in tiles]
        first_to_end = pltpu.roll(tiles[0], tail - 1, 1)
        end_to_first = pltpu.roll(tiles[-1], LANE - tail + 1, 1)
        result = []
        for c in range(n_col):
            if c < n_col - 1:
                nxt = jnp.where(lane < LANE - 1, left[c], left[c + 1])
            else:
                nxt = jnp.where(lane < tail - 1, left[c], first_to_end)
            prv = jnp.where(lane > 0, right[c], right[c - 1] if c > 0 else end_to_first)
            result.append(nxt - prv)
        return result

    def constants(j, count):
        def spread(t, i):
            return jnp.broadcast_to(t[i : i + 1, :], (count, LANE))

        return spread(cosines, j), spread(cosines, j + 2), spread(weights, j + 1)

    lane32 = iota((RANK, LANE), 1)

    def sketch_row(j):
        c_above, c_below, weight = constants(j, RANK)
        zonal = roll_pair([north_sketch[j, :, c * LANE : (c + 1) * LANE] for c in range(n_col)], lane32)
        for c in range(n_col):
            part = slice(c * LANE, (c + 1) * LANE)
            value = (zonal[c] - east_sketch[j, :, part] * c_above + east_sketch[j + 2, :, part] * c_below) * weight
            if c == n_col - 1:
                value = jnp.where(lane32 < tail, value, 0.0)
            sketch[j, :, part] = value

    lane16 = iota((16, LANE), 1)

    def field_row(j, east_above, east_below):
        c_above, c_below, weight = constants(j, 16)

        def group(g, carry):
            part = pl.ds(g * (16 * rows) + j, 16, stride=rows)
            zonal = roll_pair([north_f[c, part, :] for c in range(n_col)], lane16)
            for c in range(n_col):
                value = (zonal[c] - east_above(g, c) * c_above + east_below(g, c) * c_below) * weight
                if c == n_col - 1:
                    value = jnp.where(lane16 < tail, value, 0.0)
                field[j, pl.ds(g * 16, 16), c * LANE : (c + 1) * LANE] = value.astype(BF16)
            return carry

        lax.fori_loop(0, padded // 16, group, 0)

    def local_east(j):
        return lambda g, c: east_f[c, pl.ds(g * (16 * rows) + j, 16, stride=rows), :]

    def halo_east(side):
        return lambda g, c: edge_recv[side, pl.ds(g * 16, 16), c * LANE : (c + 1) * LANE].astype(F32)

    def widen(flat, wide):
        def run():
            for c in range(n_col):
                w = LANE if c < n_col - 1 else tail
                wide[c, 0:depth, 0:w] = flat[:, c * LANE : c * LANE + w].astype(F32)

        return run

    def send_edges():
        for side, j in ((0, 0), (1, rows - 1)):
            for c in range(n_col):
                edge_send[side, :, c * LANE : (c + 1) * LANE] = east_f[
                    c, pl.ds(j, padded, stride=rows), :
                ].astype(BF16)
        for copy in edges:
            copy.start()

    edges = [
        remote(edge_send.at[0], edge_recv.at[1], edge_ssem.at[0], edge_rsem.at[1], north),
        remote(edge_send.at[1], edge_recv.at[0], edge_ssem.at[1], edge_rsem.at[0], south),
    ]

    def field_task(j):
        if 0 < j < rows - 1:
            return lambda: field_row(j, local_east(j - 1), local_east(j + 1))
        if j == 0:
            def run():
                edges[1].wait_recv()
                field_row(0, halo_east(0), local_east(1))
        else:
            def run():
                edges[0].wait_recv()
                field_row(j, local_east(j - 1), halo_east(1))
        return run

    tasks = [widen(east_b, east_f), send_edges, widen(north_b, north_f)]
    tasks += [field_task(j) for j in list(range(1, rows - 1)) + [0, rows - 1]]

    def work(count):
        for _ in range(min(count, len(tasks))):
            tasks.pop(0)()

    far, mid, near, summed = range(4)
    reach = (4, 3, 1, 2)
    route = (2, 1, 1, 2)
    toward = (-1, 1)
    halves = (list(range(0, NSUB // 2)), list(range(NSUB // 2, NSUB)))
    pieces = (halves[1] + halves[0], halves[0] + halves[1])

    def cols(h):
        return pl.ds(h * piece, piece)

    def row_at(offset):
        return lax.rem(m + n_tm + offset, n_tm)

    def chain(side, kind, h):
        return remote(
            chain_send.at[side, kind, :, cols(h)],
            chain_recv.at[side, kind, :, cols(h)],
            chain_ssem.at[side, kind, h],
            chain_rsem.at[side, kind, h],
            z_at(toward[side] * route[kind]),
        )

    def begin(kind, edge):
        for side in (0, 1):
            j = row_at(toward[side] * reach[kind])

            def run(side=side, j=j):
                for h in halves[side] if kind == far else pieces[side]:
                    chain_send[side, kind, :, cols(h)] = sketch[j, :, cols(h)].astype(BF16)
                    chain(side, kind, h).start()

            is_edge = jnp.logical_or(j == 0, j == rows - 1)
            pl.when(is_edge if edge else jnp.logical_not(is_edge))(run)

    def relay(side):
        j = row_at(toward[side] * 2)
        for h in pieces[side]:
            value = sketch[j, :, cols(h)]
            for kind in (mid, far) if h in halves[side] else (mid,):
                chain(side, kind, h).wait_recv()
                value = value + chain_recv[side, kind, :, cols(h)].astype(F32)
            chain_send[side, summed, :, cols(h)] = value.astype(BF16)
            chain(side, summed, h).start()

    to_one, to_two, to_three, to_four = range(4)
    stride_of = (1, 2, 1, 2)

    def gather(side, kind, h, j):
        return remote(
            whole.at[j, :, cols(h)],
            whole.at[j, :, cols(h)],
            gather_ssem.at[side, kind, h],
            gather_rsem.at[side, kind, h],
            z_at(toward[side] * stride_of[kind]),
        )

    def arrive(side, kind):
        j = row_at(-toward[side] * (kind + 1))
        for h in halves[side] if kind == to_four else pieces[side]:
            gather(side, kind, h, j).wait_recv()
            if kind == to_two:
                if h in halves[side]:
                    gather(side, to_four, h, j).start()
                gather(side, to_three, h, j).start()

    def consume(j):
        projection[...] += dot_t(whole[j], field[j])

    class LatSum:
        def __init__(self, n):
            self.levels = (
                (x_slots.at[n], x_ssem.at[n], x_rsem.at[n], x * 2 + core, x_line, x_peer),
                (y_slots.at[n], y_ssem.at[n], y_rsem.at[n], y, y_line, y_peer),
            )

        def copy(self, level, i, slot):
            slots_of, ssem, rsem, _, line, _ = self.levels[level]
            return remote(slots_of.at[slot], slots_of.at[slot], ssem.at[i], rsem.at[i], line[i])

        def send(self, level, value):
            slots_of, _, _, here, line, _ = self.levels[level]
            slots_of[here] = value
            for i in range(len(line)):
                self.copy(level, i, here).start()

        def total(self, level):
            slots_of, _, _, _, line, peer_of = self.levels[level]
            for i in range(len(line)):
                self.copy(level, i, peer_of(i + 1, -1)).wait_recv()
            value = slots_of[0]
            for i in range(1, len(line) + 1):
                value = value + slots_of[i]
            return value

        def drain(self):
            for level, (_, _, _, here, line, _) in enumerate(self.levels):
                for i in range(len(line)):
                    self.copy(level, i, here).wait_send()

    def gram_copy(d, slot):
        return remote(
            gram_slots.at[slot], gram_slots.at[slot], gram_ssem.at[d - 1], gram_rsem.at[d - 1],
            {"tm": lax.rem(m + d, n_tm)},
        )

    gram_sum, projection_sum = LatSum(0), LatSum(1)
    projection[...] = jnp.zeros(projection.shape, F32)

    for j in range(1, rows - 1):
        sketch_row(j)
    for kind in (far, mid, near):
        begin(kind, False)
    for side in (0, 1):
        halos[1 - side].wait_recv()
        east_sketch[side * (rows + 1)] = halo_recv[side].astype(F32)
    for j in (0, rows - 1):
        sketch_row(j)
    for kind in (far, mid, near):
        begin(kind, True)
    work(3)
    relay(0)
    relay(1)
    work(3)
    for h in range(NSUB):
        value = sketch[m, :, cols(h)]
        for kind in (near, summed):
            for side in (0, 1):
                chain(side, kind, h).wait_recv()
                value = value + chain_recv[side, kind, :, cols(h)].astype(F32)
        whole[m, :, cols(h)] = value.astype(BF16)
        for kind in (to_two, to_one):
            for side in (0, 1):
                gather(side, kind, h, m).start()
    own = whole[m]
    gram_part[...] = jnp.zeros((RANK, LANE), F32)
    gram_part[:, 0:RANK] = dot_t(own, own)
    gram_sum.send(0, gram_part[...])
    work(2)
    arrive(0, to_two)
    arrive(1, to_two)
    gram_sum.send(1, gram_sum.total(0))
    work(len(tasks))
    for offset in (0, -2, 2):
        consume(row_at(offset))
    gram_slots[m] = gram_sum.total(1)
    for d in range(1, n_tm):
        gram_copy(d, m).start()
    for kind, offset in ((to_one, 1), (to_three, 3)):
        for side in (0, 1):
            arrive(side, kind)
            consume(row_at(-toward[side] * offset))
    arrive(0, to_four)
    arrive(1, to_four)
    consume(row_at(4))
    projection_sum.send(0, projection[...])
    for d in range(1, n_tm):
        gram_copy(d, lax.rem(m + n_tm - d, n_tm)).wait_recv()
    gram = gram_slots[0]
    for i in range(1, n_tm):
        gram = gram + gram_slots[i]
    inverse = inverse_factor(gram * (1.0 / cells))
    projection_sum.send(1, projection_sum.total(0))

    size = RANK * rows
    take_row = (iota((size, RANK), 0) // rows == iota((size, RANK), 1)).astype(F32).astype(BF16)
    take_col = (iota((RANK, size), 0) == lax.rem(iota((RANK, size), 1), RANK)).astype(F32).astype(BF16)
    same = lax.rem(iota((size, size), 0), rows) == iota((size, size), 1) // RANK
    flat = whole[...].reshape(size, width)
    basis = None
    for half in split(inverse):
        spread = dot(take_row, half).astype(BF16)
        spread = dot(spread, take_col)
        spread = jnp.where(same, spread, 0.0).astype(BF16)
        term = dot(spread, flat)
        basis = term if basis is None else basis + term
    basis_ref[...] = basis.reshape(RANK, rows, width)[:, :, :lons].astype(BF16)
    projected = projection_sum.total(1)
    coeffs = dot(inverse, projected, HIGHEST) * (1.0 / cells)
    coeffs = jnp.where(iota((RANK, padded), 1) < count_ref[0], coeffs, 0.0)
    coeffs_ref[...] = coeffs[:, :slots]

    for copy in halos + edges:
        copy.wait_send()
    for side in (0, 1):
        for kind in range(4):
            for h in range(NSUB):
                if kind != far or h in halves[side]:
                    chain(side, kind, h).wait_send()
                if kind != to_four or h in halves[side]:
                    gather(side, kind, h, m).wait_send()
    for part in (gram_sum, projection_sum):
        part.drain()
    for d in range(1, n_tm):
        gram_copy(d, m).wait_send()


def local(n_tm, n_lat, n_x, wind_east, wind_north, snap_counts, snap_ids):
    slots, rows, lons = wind_east.shape
    padded = -(-slots // LANE) * LANE
    n_col = -(-lons // LANE)
    width = n_col * LANE
    n_y = n_lat // (2 * n_x)
    ids = snap_ids.reshape(1, slots)
    shape = (slots, rows, lons, n_tm, n_lat, n_x)
    dma = pltpu.SemaphoreType.DMA
    return pl.pallas_call(
        functools.partial(kernel, shape),
        out_shape=(
            jax.ShapeDtypeStruct((RANK, rows, lons), BF16),
            jax.ShapeDtypeStruct((RANK, slots), F32),
        ),
        in_specs=[
            pl.BlockSpec(memory_space=pl.ANY),
            pl.BlockSpec(memory_space=pl.ANY),
            pl.BlockSpec(memory_space=pltpu.SMEM),
            pl.BlockSpec(memory_space=pltpu.VMEM),
        ],
        out_specs=(pl.BlockSpec(memory_space=pltpu.VMEM), pl.BlockSpec(memory_space=pltpu.VMEM)),
        scratch_shapes=[
            pltpu.VMEM((n_col, padded * rows, LANE), F32),
            pltpu.VMEM((n_col, padded * rows, LANE), F32),
            pltpu.VMEM((slots * rows, lons), BF16),
            pltpu.VMEM((slots * rows, lons), BF16),
            pltpu.VMEM((rows * RANK, slots * rows), BF16),
            pltpu.VMEM((rows + 2, RANK, width), F32),
            pltpu.VMEM((rows, RANK, width), F32),
            pltpu.VMEM((rows, RANK, width), F32),
            pltpu.VMEM((2, RANK, width), BF16),
            pltpu.VMEM((2, RANK, width), BF16),
            pltpu.VMEM((2, padded, width), BF16),
            pltpu.VMEM((2, padded, width), BF16),
            pltpu.VMEM((rows, padded, width), BF16),
            pltpu.VMEM((2, 4, RANK, width), BF16),
            pltpu.VMEM((2, 4, RANK, width), BF16),
            pltpu.VMEM((rows, RANK, width), BF16),
            pltpu.VMEM((RANK, padded), F32),
            pltpu.VMEM((RANK, LANE), F32),
            pltpu.VMEM((n_tm, RANK, LANE), F32),
            pltpu.VMEM((2, 2 * n_x, RANK, LANE), F32),
            pltpu.VMEM((2, n_y, RANK, LANE), F32),
            dma((2,)),
            dma((2,)),
            dma((2,)),
            dma((2,)),
            dma((2,)),
            dma((2, 4, NSUB)),
            dma((2, 4, NSUB)),
            dma((2, 4, NSUB)),
            dma((2, 4, NSUB)),
            dma((n_tm - 1,)),
            dma((n_tm - 1,)),
            dma((2, 2 * n_x - 1)),
            dma((2, 2 * n_x - 1)),
            dma((2, n_y - 1)),
            dma((2, n_y - 1)),
        ],
        compiler_params=pltpu.CompilerParams(
            collective_id=0, has_side_effects=True, vmem_limit_bytes=60 * 1024 * 1024
        ),
        name="eof",
    )(
        wind_east.reshape(slots * rows, lons), wind_north.reshape(slots * rows, lons), snap_counts, ids
    )


def solution(mesh):
    in_specs = (P("tm", "lat", None), P("tm", "lat", None), P("tm"), P("tm"))
    out_specs = (P(None, "lat", None), P(None, "tm"))
    body = functools.partial(local, mesh.shape["tm"], mesh.shape["lat"], 4)
    return jax.shard_map(body, mesh=mesh, in_specs=in_specs, out_specs=out_specs, check_vma=False)
```

time: 67.1 us -> 56.7 us (0.85)
  Pallas kernels: 61.1 us -> 51.9 us
  local copies, waits for them, and re-layouts: 4.55 us -> 3.39 us
    pallas_call x1, Pallas kernels: 61.1 us -> 51.9 us  [local(): pl.pallas_call(functools.partial(kernel, shape), out_shape=(jax.ShapeDtyp...]
    reshape x1 -> x0, local copies, waits for them, and re-layouts: 1.17 us -> none  [local(): ids = jnp.pad(snap_ids, (0, padded - slots)).reshape(1, padded)]
where the time goes in v3:
time: 56.7 us; the launch traced here: 56.5 us
  Pallas kernels  51.9 us (92%)
  local copies, waits for them, and re-layouts  3.39 us (6%)
  between operations  1.28 us (2%)
    pallas_call x1, Pallas kernels, local(): pl.pallas_call(functools.partial(kernel, shape), out_shape=(jax.ShapeDtyp...  51.9 us
    unnamed x2, local copies, waits for them, and re-layouts  3.39 us

profile of v3, /device:TPU:1, one launch (start us, length us, event | category | flops | bytes accessed | tf_op | source)
XLA Modules:
  0.0 56.5 jit_solution(770274978898632537)
XLA Ops:
  1.3 51.9 %eof.1 = (bf16[32,8,1440]{2,1,0:T(8,128)(2,1)}, f32[32,120]{1,0:T(8,128)}) custom-call(bf16[960,1440]{1,0:T(8,128)(2,1)} %bitcast.3, bf16[960,1440]{1,0:T(8,128)(2,1)} %bitcast.4, s32[1]{0:T(128)S(6)} %copy.8.count_ref, s32[1,120]{1,0:T(1,128)} %bitcast.5), custom_call_target="tpu_custom_call" | custom-call | tf_op jit(solution)/shard_map/eof/pallas_call | solution.py:496
  53.1 2.1 %copy.9 = bf16[32,8,1440]{2,1,0:T(8,128)(2,1)} copy(bf16[32,8,1440]{2,1,0:T(8,128)(2,1)} %get-tuple-element.4) | data formatting | bytes 1474560
  55.2 1.3 %copy.10 = f32[32,120]{1,0:T(8,128)} copy(f32[32,120]{1,0:T(8,128)} %get-tuple-element.5) | data formatting | bytes 30720

commit v4 on v3

--- a/solution.py
+++ b/solution.py
@@ -293,7 +293,8 @@
     route = (2, 1, 1, 2)
     toward = (-1, 1)
     halves = (list(range(0, NSUB // 2)), list(range(NSUB // 2, NSUB)))
-    pieces = (halves[1] + halves[0], halves[0] + halves[1])
+    order = [h for pair in zip(halves[0], halves[1]) for h in pair]
+    pieces = ([h for pair in zip(halves[1], halves[0]) for h in pair], order)
 
     def cols(h):
         return pl.ds(h * piece, piece)
@@ -310,27 +311,54 @@
             z_at(toward[side] * route[kind]),
         )
 
-    def begin(kind, edge):
+    def send_own(side, kind, h):
+        j = row_at(toward[side] * reach[kind])
+        chain_send[side, kind, :, cols(h)] = sketch[j, :, cols(h)].astype(BF16)
+        chain(side, kind, h).start()
+
+    def when_class(edge, offset, run):
+        j = row_at(offset)
+        is_edge = jnp.logical_or(j == 0, j == rows - 1)
+        pl.when(is_edge if edge else jnp.logical_not(is_edge))(run)
+
+    def begin(edge):
+        for step in range(NSUB // 2):
+            first = [pieces[side][2 * step] for side in (0, 1)]
+            second = [pieces[side][2 * step + 1] for side in (0, 1)]
+            for side in (0, 1):
+                when_class(edge, toward[side] * reach[mid], lambda side=side: send_own(side, mid, first[side]))
+
+            def send_far():
+                for side in (0, 1):
+                    send_own(side, far, second[side])
+
+            when_class(edge, reach[far], send_far)
+            for side in (0, 1):
+                when_class(edge, toward[side] * reach[mid], lambda side=side: send_own(side, mid, second[side]))
+
+    def begin_near(edge):
         for side in (0, 1):
-            j = row_at(toward[side] * reach[kind])
-
-            def run(side=side, j=j):
-                for h in halves[side] if kind == far else pieces[side]:
-                    chain_send[side, kind, :, cols(h)] = sketch[j, :, cols(h)].astype(BF16)
-                    chain(side, kind, h).start()
-
-            is_edge = jnp.logical_or(j == 0, j == rows - 1)
-            pl.when(is_edge if edge else jnp.logical_not(is_edge))(run)
-
-    def relay(side):
-        j = row_at(toward[side] * 2)
-        for h in pieces[side]:
-            value = sketch[j, :, cols(h)]
-            for kind in (mid, far) if h in halves[side] else (mid,):
-                chain(side, kind, h).wait_recv()
-                value = value + chain_recv[side, kind, :, cols(h)].astype(F32)
-            chain_send[side, summed, :, cols(h)] = value.astype(BF16)
-            chain(side, summed, h).start()
+
+            def run(side=side):
+                for h in order:
+                    send_own(side, near, h)
+
+            when_class(edge, toward[side] * reach[near], run)
+
+    def relay(edge):
+        for i in range(NSUB):
+            for side in (0, 1):
+
+                def run(h=pieces[side][i], side=side):
+                    j = row_at(toward[side] * 2)
+                    value = sketch[j, :, cols(h)]
+                    for kind in (mid, far) if h in halves[side] else (mid,):
+                        chain(side, kind, h).wait_recv()
+                        value = value + chain_recv[side, kind, :, cols(h)].astype(F32)
+                    chain_send[side, summed, :, cols(h)] = value.astype(BF16)
+                    chain(side, summed, h).start()
+
+                when_class(edge, toward[side] * 2, run)
 
     to_one, to_two, to_three, to_four = range(4)
     stride_of = (1, 2, 1, 2)
@@ -344,14 +372,21 @@
             z_at(toward[side] * stride_of[kind]),
         )
 
-    def arrive(side, kind):
-        j = row_at(-toward[side] * (kind + 1))
-        for h in halves[side] if kind == to_four else pieces[side]:
-            gather(side, kind, h, j).wait_recv()
-            if kind == to_two:
-                if h in halves[side]:
-                    gather(side, to_four, h, j).start()
-                gather(side, to_three, h, j).start()
+    def arrive(kind, edge):
+        for h in order:
+            for side in (0, 1):
+                if kind == to_four and h not in halves[side]:
+                    continue
+
+                def run(h=h, side=side):
+                    j = row_at(-toward[side] * (kind + 1))
+                    gather(side, kind, h, j).wait_recv()
+                    if kind == to_two:
+                        if h in halves[side]:
+                            gather(side, to_four, h, j).start()
+                        gather(side, to_three, h, j).start()
+
+                when_class(edge, -toward[side] * (kind + 1), run)
 
     def consume(j):
         projection[...] += dot_t(whole[j], field[j])
@@ -398,37 +433,42 @@
 
     for j in range(1, rows - 1):
         sketch_row(j)
-    for kind in (far, mid, near):
-        begin(kind, False)
+    begin(False)
+    work(3)
     for side in (0, 1):
         halos[1 - side].wait_recv()
         east_sketch[side * (rows + 1)] = halo_recv[side].astype(F32)
     for j in (0, rows - 1):
         sketch_row(j)
-    for kind in (far, mid, near):
-        begin(kind, True)
-    work(3)
-    relay(0)
-    relay(1)
-    work(3)
-    for h in range(NSUB):
+    begin(True)
+    begin_near(False)
+    work(1)
+    relay(False)
+    begin_near(True)
+    work(1)
+    relay(True)
+    work(2)
+    for h in order:
         value = sketch[m, :, cols(h)]
         for kind in (near, summed):
             for side in (0, 1):
                 chain(side, kind, h).wait_recv()
                 value = value + chain_recv[side, kind, :, cols(h)].astype(F32)
         whole[m, :, cols(h)] = value.astype(BF16)
-        for kind in (to_two, to_one):
-            for side in (0, 1):
-                gather(side, kind, h, m).start()
+        for side in (0, 1):
+            gather(side, to_two, h, m).start()
+    for h in order:
+        for side in (0, 1):
+            gather(side, to_one, h, m).start()
     own = whole[m]
     gram_part[...] = jnp.zeros((RANK, LANE), F32)
     gram_part[:, 0:RANK] = dot_t(own, own)
     gram_sum.send(0, gram_part[...])
     work(2)
-    arrive(0, to_two)
-    arrive(1, to_two)
     gram_sum.send(1, gram_sum.total(0))
+    arrive(to_two, False)
+    work(1)
+    arrive(to_two, True)
     work(len(tasks))
     for offset in (0, -2, 2):
         consume(row_at(offset))
@@ -436,11 +476,12 @@
     for d in range(1, n_tm):
         gram_copy(d, m).start()
     for kind, offset in ((to_one, 1), (to_three, 3)):
+        for edge in (False, True):
+            arrive(kind, edge)
         for side in (0, 1):
-            arrive(side, kind)
             consume(row_at(-toward[side] * offset))
-    arrive(0, to_four)
-    arrive(1, to_four)
+    for edge in (False, True):
+        arrive(to_four, edge)
     consume(row_at(4))
     projection_sum.send(0, projection[...])
     for d in range(1, n_tm):
@@ -484,6 +525,11 @@
         gram_copy(d, m).wait_send()
 
 
+def write_kernel(basis_ref, coeffs_ref, basis_out, coeffs_out):
+    basis_out[...] = basis_ref[...]
+    coeffs_out[...] = coeffs_ref[...]
+
+
 def local(n_tm, n_lat, n_x, wind_east, wind_north, snap_counts, snap_ids):
     slots, rows, lons = wind_east.shape
     padded = -(-slots // LANE) * LANE
@@ -493,12 +539,11 @@
     ids = snap_ids.reshape(1, slots)
     shape = (slots, rows, lons, n_tm, n_lat, n_x)
     dma = pltpu.SemaphoreType.DMA
-    return pl.pallas_call(
+    in_vmem = pl.BlockSpec(memory_space=pltpu.VMEM)
+    results = (jax.ShapeDtypeStruct((RANK, rows, lons), BF16), jax.ShapeDtypeStruct((RANK, slots), F32))
+    found = pl.pallas_call(
         functools.partial(kernel, shape),
-        out_shape=(
-            jax.ShapeDtypeStruct((RANK, rows, lons), BF16),
-            jax.ShapeDtypeStruct((RANK, slots), F32),
-        ),
+        out_shape=results,
         in_specs=[
             pl.BlockSpec(memory_space=pl.ANY),
             pl.BlockSpec(memory_space=pl.ANY),
@@ -551,6 +596,9 @@
     )(
         wind_east.reshape(slots * rows, lons), wind_north.reshape(slots * rows, lons), snap_counts, ids
     )
+    return pl.pallas_call(
+        write_kernel, out_shape=results, in_specs=[in_vmem, in_vmem], out_specs=(in_vmem, in_vmem), name="write"
+    )(*found)
 
 
 def solution(mesh):

time: 56.7 us -> 55.4 us (0.977)
  local copies, waits for them, and re-layouts: 3.39 us -> 0 us
  Pallas kernels: 51.9 us -> 54 us
    unnamed x2 -> x0, local copies, waits for them, and re-layouts: 3.39 us -> none
    pallas_call x1 -> x2, Pallas kernels: 51.9 us -> 54 us  [the longest x1 51.9 us: local(): pl.pallas_call(functools.partial(kernel, shape), out_shape=results, in_sp...]
where the time goes in v4:
time: 55.4 us; the launch traced here: 55.3 us
  Pallas kernels  54 us (97%)
  between operations  1.28 us (2%)
    pallas_call x1, Pallas kernels, local(): pl.pallas_call(functools.partial(kernel, shape), out_shape=results, in_sp...  51.9 us
    pallas_call x1, Pallas kernels, local(): pl.pallas_call(write_kernel, out_shape=results, in_specs=[in_vmem, in_vme...  2.07 us

profile of v4, /device:TPU:1, one launch (start us, length us, event | category | flops | bytes accessed | tf_op | source)
XLA Modules:
  0.0 55.3 jit_solution(6368417049332226676)
XLA Ops:
  1.3 51.9 %eof.1 = (bf16[32,8,1440]{2,1,0:T(8,128)(2,1)}, f32[32,120]{1,0:T(8,128)}) custom-call(bf16[960,1440]{1,0:T(8,128)(2,1)} %bitcast.3, bf16[960,1440]{1,0:T(8,128)(2,1)} %bitcast.4, s32[1]{0:T(128)S(6)} %copy.6.count_ref, s32[1,120]{1,0:T(1,128)} %bitcast.5), custom_call_target="tpu_custom_call" | custom-call | tf_op jit(solution)/shard_map/eof/pallas_call | solution.py:544
  53.2 2.1 %write.1 = (bf16[32,8,1440]{2,1,0:T(8,128)(2,1)}, f32[32,120]{1,0:T(8,128)}) custom-call(bf16[32,8,1440]{2,1,0:T(8,128)(2,1)} %get-tuple-element.4.basis_ref, f32[32,120]{1,0:T(8,128)} %get-tuple-element.5.coeffs_ref), custom_call_target="tpu_custom_call" | custom-call | tf_op jit(solution)/shard_map/write/pallas_call | solution.py:599

commit v5 on v4

--- a/solution.py
+++ b/solution.py
@@ -63,7 +63,7 @@
     shape,
     east_hbm,
     north_hbm,
-    count_ref,
+    count_hbm,
     ids_ref,
     basis_ref,
     coeffs_ref,
@@ -88,6 +88,7 @@
     gram_slots,
     x_slots,
     y_slots,
+    count_ref,
     load_sem,
     halo_ssem,
     halo_rsem,
@@ -144,12 +145,14 @@
             src_ref=src, dst_ref=dst, send_sem=ssem, recv_sem=rsem, device_id=peer, device_id_type=MESH
         )
 
-    loads = [
-        pltpu.make_async_copy(east_hbm, east_b, load_sem.at[0]),
-        pltpu.make_async_copy(north_hbm, north_b, load_sem.at[1]),
-    ]
+    middle = slots * rows // 2
+    ends = [slice(0, middle), slice(middle, slots * rows)]
+    loads = [pltpu.make_async_copy(count_hbm, count_ref, load_sem.at[3])]
+    loads += [pltpu.make_async_copy(east_hbm.at[part], east_b.at[part], load_sem.at[i]) for i, part in enumerate(ends)]
+    loads += [pltpu.make_async_copy(north_hbm, north_b, load_sem.at[2])]
     for copy in loads:
         copy.start()
+    loads[0].wait()
 
     ids = jnp.broadcast_to(ids_ref[...], (RANK, slots))
     column = iota((RANK, slots), 0)
@@ -176,8 +179,12 @@
     for wide in (east_f, north_f):
         wide[:, depth:, :] = jnp.zeros((n_col, padded * rows - depth, LANE), F32)
 
-    loads[0].wait()
-    east_sketch[1 : rows + 1, :, 0:lons] = dot(spread_signs[...], east_b[...]).reshape(rows, RANK, lons)
+    for i, part in enumerate(ends):
+        loads[1 + i].wait()
+        partial = dot(spread_signs[:, part], east_b[part, :]).reshape(rows, RANK, lons)
+        if i > 0:
+            partial = east_sketch[1 : rows + 1, :, 0:lons] + partial
+        east_sketch[1 : rows + 1, :, 0:lons] = partial
     for side, j in ((0, 1), (1, rows)):
         halo_send[side] = east_sketch[j].astype(BF16)
     pl.semaphore_wait(barrier, len(peers))
@@ -187,7 +194,7 @@
     ]
     for copy in halos:
         copy.start()
-    loads[1].wait()
+    loads[3].wait()
     north_sketch[:, :, 0:lons] = dot(spread_signs[...], north_b[...]).reshape(rows, RANK, lons)
 
     def roll_pair(tiles, lane):
@@ -465,8 +472,8 @@
     gram_part[:, 0:RANK] = dot_t(own, own)
     gram_sum.send(0, gram_part[...])
     work(2)
+    arrive(to_two, False)
     gram_sum.send(1, gram_sum.total(0))
-    arrive(to_two, False)
     work(1)
     arrive(to_two, True)
     work(len(tasks))
@@ -525,11 +532,6 @@
         gram_copy(d, m).wait_send()
 
 
-def write_kernel(basis_ref, coeffs_ref, basis_out, coeffs_out):
-    basis_out[...] = basis_ref[...]
-    coeffs_out[...] = coeffs_ref[...]
-
-
 def local(n_tm, n_lat, n_x, wind_east, wind_north, snap_counts, snap_ids):
     slots, rows, lons = wind_east.shape
     padded = -(-slots // LANE) * LANE
@@ -539,15 +541,13 @@
     ids = snap_ids.reshape(1, slots)
     shape = (slots, rows, lons, n_tm, n_lat, n_x)
     dma = pltpu.SemaphoreType.DMA
-    in_vmem = pl.BlockSpec(memory_space=pltpu.VMEM)
-    results = (jax.ShapeDtypeStruct((RANK, rows, lons), BF16), jax.ShapeDtypeStruct((RANK, slots), F32))
-    found = pl.pallas_call(
+    return pl.pallas_call(
         functools.partial(kernel, shape),
-        out_shape=results,
+        out_shape=(pltpu.VMEM((RANK, rows, lons), BF16), pltpu.VMEM((RANK, slots), F32)),
         in_specs=[
             pl.BlockSpec(memory_space=pl.ANY),
             pl.BlockSpec(memory_space=pl.ANY),
-            pl.BlockSpec(memory_space=pltpu.SMEM),
+            pl.BlockSpec(memory_space=pltpu.HBM),
             pl.BlockSpec(memory_space=pltpu.VMEM),
         ],
         out_specs=(pl.BlockSpec(memory_space=pltpu.VMEM), pl.BlockSpec(memory_space=pltpu.VMEM)),
@@ -573,7 +573,8 @@
             pltpu.VMEM((n_tm, RANK, LANE), F32),
             pltpu.VMEM((2, 2 * n_x, RANK, LANE), F32),
             pltpu.VMEM((2, n_y, RANK, LANE), F32),
-            dma((2,)),
+            pltpu.SMEM((1,), jnp.int32),
+            dma((4,)),
             dma((2,)),
             dma((2,)),
             dma((2,)),
@@ -596,9 +597,6 @@
     )(
         wind_east.reshape(slots * rows, lons), wind_north.reshape(slots * rows, lons), snap_counts, ids
     )
-    return pl.pallas_call(
-        write_kernel, out_shape=results, in_specs=[in_vmem, in_vmem], out_specs=(in_vmem, in_vmem), name="write"
-    )(*found)
 
 
 def solution(mesh):

time: 55.4 us -> 53 us (0.957)
  the two profiles are of different devices: /device:TPU:1 before, /device:TPU:4 now
where the time goes in v5:
time: 53 us; the launch traced here: 52.9 us
  Pallas kernels  50.1 us (95%)
  local copies, waits for them, and re-layouts  1.49 us (3%)
  between operations  1.28 us (2%)
    pallas_call x1, Pallas kernels, local(): pl.pallas_call(functools.partial(kernel, shape), out_shape=(pltpu.VMEM((R...  50.1 us
    unnamed x2, local copies, waits for them, and re-layouts  1.49 us

profile of v5, /device:TPU:4, one launch (start us, length us, event | category | flops | bytes accessed | tf_op | source)
XLA Modules:
  0.0 52.9 jit_solution(6455281742493791337)
XLA Ops:
  1.3 50.1 %eof.1 = (bf16[32,8,1440]{2,1,0:T(8,128)(2,1)S(1)}, f32[32,120]{1,0:T(8,128)S(1)}) custom-call(bf16[960,1440]{1,0:T(8,128)(2,1)} %bitcast.3, bf16[960,1440]{1,0:T(8,128)(2,1)} %bitcast.4, s32[1]{0:T(128)S(6)} %copy.10.count_hbm, s32[1,120]{1,0:T(1,128)} %bitcast.5), custom_call_target="tpu_custom_call" | custom-call | tf_op jit(solution)/shard_map/eof/pallas_call | solution.py:544
  51.4 0.9 %copy.8 = bf16[32,8,1440]{2,1,0:T(8,128)(2,1)} copy(bf16[32,8,1440]{2,1,0:T(8,128)(2,1)S(1)} %get-tuple-element.2) | data formatting | bytes 1474560
  52.3 0.6 %copy.9 = f32[32,120]{1,0:T(8,128)} copy(f32[32,120]{1,0:T(8,128)S(1)} %get-tuple-element.3) | data formatting | bytes 30720

commit v6 on v5

--- a/solution.py
+++ b/solution.py
@@ -86,8 +86,10 @@
     projection,
     gram_part,
     gram_slots,
-    x_slots,
-    y_slots,
+    gram_x,
+    gram_y,
+    projection_x,
+    projection_y,
     count_ref,
     load_sem,
     halo_ssem,
@@ -188,12 +190,25 @@
     for side, j in ((0, 1), (1, rows)):
         halo_send[side] = east_sketch[j].astype(BF16)
     pl.semaphore_wait(barrier, len(peers))
-    halos = [
-        remote(halo_send.at[0], halo_recv.at[1], halo_ssem.at[0], halo_rsem.at[1], north),
-        remote(halo_send.at[1], halo_recv.at[0], halo_ssem.at[1], halo_rsem.at[0], south),
-    ]
-    for copy in halos:
-        copy.start()
+
+    def cols(h):
+        return pl.ds(h * piece, piece)
+
+    halves = (list(range(0, NSUB // 2)), list(range(NSUB // 2, NSUB)))
+    order = [h for pair in zip(halves[0], halves[1]) for h in pair]
+
+    def halo(side, h):
+        return remote(
+            halo_send.at[side, :, cols(h)],
+            halo_recv.at[1 - side, :, cols(h)],
+            halo_ssem.at[side, h],
+            halo_rsem.at[1 - side, h],
+            (north, south)[side],
+        )
+
+    for h in order:
+        for side in (0, 1):
+            halo(side, h).start()
     loads[3].wait()
     north_sketch[:, :, 0:lons] = dot(spread_signs[...], north_b[...]).reshape(rows, RANK, lons)
 
@@ -225,10 +240,27 @@
         zonal = roll_pair([north_sketch[j, :, c * LANE : (c + 1) * LANE] for c in range(n_col)], lane32)
         for c in range(n_col):
             part = slice(c * LANE, (c + 1) * LANE)
-            value = (zonal[c] - east_sketch[j, :, part] * c_above + east_sketch[j + 2, :, part] * c_below) * weight
+            value = zonal[c]
+            if j > 0:
+                value = value - east_sketch[j, :, part] * c_above
+            if j < rows - 1:
+                value = value + east_sketch[j + 2, :, part] * c_below
+            value = value * weight
             if c == n_col - 1:
                 value = jnp.where(lane32 < tail, value, 0.0)
             sketch[j, :, part] = value
+
+    def add_halo(side, h):
+        halo(1 - side, h).wait_recv()
+        j = (0, rows - 1)[side]
+        c_above, c_below, weight = constants(j, RANK)
+        scale = (-c_above * weight, c_below * weight)[side]
+        for c in range(h * (piece // LANE), (h + 1) * (piece // LANE)):
+            part = slice(c * LANE, (c + 1) * LANE)
+            value = halo_recv[side, :, part].astype(F32) * scale
+            if c == n_col - 1:
+                value = jnp.where(lane32 < tail, value, 0.0)
+            sketch[j, :, part] += value
 
     lane16 = iota((16, LANE), 1)
 
@@ -299,12 +331,7 @@
     reach = (4, 3, 1, 2)
     route = (2, 1, 1, 2)
     toward = (-1, 1)
-    halves = (list(range(0, NSUB // 2)), list(range(NSUB // 2, NSUB)))
-    order = [h for pair in zip(halves[0], halves[1]) for h in pair]
     pieces = ([h for pair in zip(halves[1], halves[0]) for h in pair], order)
-
-    def cols(h):
-        return pl.ds(h * piece, piece)
 
     def row_at(offset):
         return lax.rem(m + n_tm + offset, n_tm)
@@ -330,6 +357,10 @@
 
     def begin(edge):
         for step in range(NSUB // 2):
+            if edge:
+                for h in order[2 * step : 2 * step + 2]:
+                    for side in (0, 1):
+                        add_halo(side, h)
             first = [pieces[side][2 * step] for side in (0, 1)]
             second = [pieces[side][2 * step + 1] for side in (0, 1)]
             for side in (0, 1):
@@ -399,10 +430,10 @@
         projection[...] += dot_t(whole[j], field[j])
 
     class LatSum:
-        def __init__(self, n):
+        def __init__(self, n, x_slots, y_slots):
             self.levels = (
-                (x_slots.at[n], x_ssem.at[n], x_rsem.at[n], x * 2 + core, x_line, x_peer),
-                (y_slots.at[n], y_ssem.at[n], y_rsem.at[n], y, y_line, y_peer),
+                (x_slots, x_ssem.at[n], x_rsem.at[n], x * 2 + core, x_line, x_peer),
+                (y_slots, y_ssem.at[n], y_rsem.at[n], y, y_line, y_peer),
             )
 
         def copy(self, level, i, slot):
@@ -411,7 +442,7 @@
 
         def send(self, level, value):
             slots_of, _, _, here, line, _ = self.levels[level]
-            slots_of[here] = value
+            slots_of[here] = value.astype(slots_of.dtype)
             for i in range(len(line)):
                 self.copy(level, i, here).start()
 
@@ -419,9 +450,9 @@
             slots_of, _, _, _, line, peer_of = self.levels[level]
             for i in range(len(line)):
                 self.copy(level, i, peer_of(i + 1, -1)).wait_recv()
-            value = slots_of[0]
+            value = slots_of[0].astype(F32)
             for i in range(1, len(line) + 1):
-                value = value + slots_of[i]
+                value = value + slots_of[i].astype(F32)
             return value
 
         def drain(self):
@@ -435,18 +466,15 @@
             {"tm": lax.rem(m + d, n_tm)},
         )
 
-    gram_sum, projection_sum = LatSum(0), LatSum(1)
+    gram_sum, projection_sum = LatSum(0, gram_x, gram_y), LatSum(1, projection_x, projection_y)
     projection[...] = jnp.zeros(projection.shape, F32)
 
     for j in range(1, rows - 1):
         sketch_row(j)
     begin(False)
-    work(3)
-    for side in (0, 1):
-        halos[1 - side].wait_recv()
-        east_sketch[side * (rows + 1)] = halo_recv[side].astype(F32)
     for j in (0, rows - 1):
         sketch_row(j)
+    work(3)
     begin(True)
     begin_near(False)
     work(1)
@@ -517,8 +545,11 @@
     coeffs = jnp.where(iota((RANK, padded), 1) < count_ref[0], coeffs, 0.0)
     coeffs_ref[...] = coeffs[:, :slots]
 
-    for copy in halos + edges:
+    for copy in edges:
         copy.wait_send()
+    for side in (0, 1):
+        for h in range(NSUB):
+            halo(side, h).wait_send()
     for side in (0, 1):
         for kind in range(4):
             for h in range(NSUB):
@@ -571,12 +602,14 @@
             pltpu.VMEM((RANK, padded), F32),
             pltpu.VMEM((RANK, LANE), F32),
             pltpu.VMEM((n_tm, RANK, LANE), F32),
-            pltpu.VMEM((2, 2 * n_x, RANK, LANE), F32),
-            pltpu.VMEM((2, n_y, RANK, LANE), F32),
+            pltpu.VMEM((2 * n_x, RANK, LANE), F32),
+            pltpu.VMEM((n_y, RANK, LANE), F32),
+            pltpu.VMEM((2 * n_x, RANK, padded), BF16),
+            pltpu.VMEM((n_y, RANK, padded), BF16),
             pltpu.SMEM((1,), jnp.int32),
             dma((4,)),
-            dma((2,)),
-            dma((2,)),
+            dma((2, NSUB)),
+            dma((2, NSUB)),
             dma((2,)),
             dma((2,)),
             dma((2, 4, NSUB)),

time: 53 us -> 52.1 us (0.983)
  the two profiles are of different devices: /device:TPU:4 before, /device:TPU:1 now
where the time goes in v6:
time: 52.1 us; the launch traced here: 51.3 us
  Pallas kernels  48.5 us (93%)
  local copies, waits for them, and re-layouts  1.49 us (3%)
  between operations  1.28 us (2%)
    pallas_call x1, Pallas kernels, local(): pl.pallas_call(functools.partial(kernel, shape), out_shape=(pltpu.VMEM((R...  48.5 us
    unnamed x2, local copies, waits for them, and re-layouts  1.49 us

profile of v6, /device:TPU:1, one launch (start us, length us, event | category | flops | bytes accessed | tf_op | source)
XLA Modules:
  0.0 51.3 jit_solution(12550783513950793630)
XLA Ops:
  1.3 48.5 %eof.1 = (bf16[32,8,1440]{2,1,0:T(8,128)(2,1)S(1)}, f32[32,120]{1,0:T(8,128)S(1)}) custom-call(bf16[960,1440]{1,0:T(8,128)(2,1)} %bitcast.3, bf16[960,1440]{1,0:T(8,128)(2,1)} %bitcast.4, s32[1]{0:T(128)S(6)} %copy.10.count_hbm, s32[1,120]{1,0:T(1,128)} %bitcast.5), custom_call_target="tpu_custom_call" | custom-call | tf_op jit(solution)/shard_map/eof/pallas_call | solution.py:575
  49.8 0.9 %copy.8 = bf16[32,8,1440]{2,1,0:T(8,128)(2,1)} copy(bf16[32,8,1440]{2,1,0:T(8,128)(2,1)S(1)} %get-tuple-element.2) | data formatting | bytes 1474560
  50.6 0.6 %copy.9 = f32[32,120]{1,0:T(8,128)} copy(f32[32,120]{1,0:T(8,128)S(1)} %get-tuple-element.3) | data formatting | bytes 30720

commit v7 on v6

--- a/solution.py
+++ b/solution.py
@@ -46,14 +46,18 @@
     return p
 
 
-def inverse_factor(gram):
-    row, lane = iota((RANK, LANE), 0), iota((RANK, LANE), 1)
-    a = jnp.where(lane == row + RANK, 1.0, gram)
-    for k in range(RANK - 1):
+def eliminate(a, steps):
+    row = iota((RANK, LANE), 0)
+    for k in steps:
         pivot_row = a[k : k + 1, :]
         column = a[:, k : k + 1]
         factor = column / a[k : k + 1, k : k + 1]
         a = a - jnp.where(row > k, factor * pivot_row, 0.0)
+    return a
+
+
+def inverse_factor(a):
+    row, lane = iota((RANK, LANE), 0), iota((RANK, LANE), 1)
     diagonal = jnp.sum(jnp.where(row == lane, a, 0.0), axis=1, keepdims=True)
     scaled = a * lax.rsqrt(diagonal)
     return pltpu.roll(scaled, LANE - RANK, 1)[:, :RANK]
@@ -524,8 +528,11 @@
     gram = gram_slots[0]
     for i in range(1, n_tm):
         gram = gram + gram_slots[i]
-    inverse = inverse_factor(gram * (1.0 / cells))
+    early = 14
+    joined = jnp.where(iota((RANK, LANE), 1) == iota((RANK, LANE), 0) + RANK, 1.0, gram * (1.0 / cells))
+    joined = eliminate(joined, range(early))
     projection_sum.send(1, projection_sum.total(0))
+    inverse = inverse_factor(eliminate(joined, range(early, RANK - 1)))
 
     size = RANK * rows
     take_row = (iota((size, RANK), 0) // rows == iota((size, RANK), 1)).astype(F32).astype(BF16)

time: 52.1 us -> 52.8 us (1.013); the launches traced: 51.3 us -> 52.7 us
  Pallas kernels: 48.5 us -> 50 us
    pallas_call x1, Pallas kernels: 48.5 us -> 50 us  [local(): pl.pallas_call(functools.partial(kernel, shape), out_shape=(pltpu.VMEM((R...]
where the time goes in v7:
time: 52.8 us; the launch traced here: 52.7 us
  Pallas kernels  50 us (95%)
  local copies, waits for them, and re-layouts  1.49 us (3%)
  between operations  1.28 us (2%)
    pallas_call x1, Pallas kernels, local(): pl.pallas_call(functools.partial(kernel, shape), out_shape=(pltpu.VMEM((R...  50 us
    unnamed x2, local copies, waits for them, and re-layouts  1.49 us

profile of v7, /device:TPU:1, one launch (start us, length us, event | category | flops | bytes accessed | tf_op | source)
XLA Modules:
  0.0 52.7 jit_solution(13276769405742594624)
XLA Ops:
  1.3 50.0 %eof.1 = (bf16[32,8,1440]{2,1,0:T(8,128)(2,1)S(1)}, f32[32,120]{1,0:T(8,128)S(1)}) custom-call(bf16[960,1440]{1,0:T(8,128)(2,1)} %bitcast.3, bf16[960,1440]{1,0:T(8,128)(2,1)} %bitcast.4, s32[1]{0:T(128)S(6)} %copy.10.count_hbm, s32[1,120]{1,0:T(1,128)} %bitcast.5), custom_call_target="tpu_custom_call" | custom-call | tf_op jit(solution)/shard_map/eof/pallas_call | solution.py:582
  51.3 0.9 %copy.8 = bf16[32,8,1440]{2,1,0:T(8,128)(2,1)} copy(bf16[32,8,1440]{2,1,0:T(8,128)(2,1)S(1)} %get-tuple-element.2) | data formatting | bytes 1474560
  52.1 0.6 %copy.9 = f32[32,120]{1,0:T(8,128)} copy(f32[32,120]{1,0:T(8,128)S(1)} %get-tuple-element.3) | data formatting | bytes 30720
